TPU v7x, 512 devices: a whole 4x4x16 slice. The times are simulated.
512 devices in a mesh: grp: 16 (over z_lo, y), row: 32 (over z_hi, x, core).
Axes of the slice: x: 4, y: 4, z: 16 (z_hi: 4, z_lo: 4; z = z_hi * 4 + z_lo), core: 2. Of those that a mesh axis runs over, the one named last changes fastest.
Arguments:
- colatitude: float32 [1048576], P(('grp', 'row')), may hold values from 0.05 to 3.09
- longitude: float32 [1048576], P(('grp', 'row')), may hold values from -3.140625 to 3.140625
- observed: bfloat16 [2, 1048576], P(None, ('grp', 'row')), may hold values from -6 to 6
- filter_taps: bfloat16 [2, 256], replicated, may hold values from -0.375 to 0.375
- segment_start: int32 [1048576], P(('grp', 'row')), may hold values 0 or 1
- harmonic: int32 [2, 512], replicated, may hold values from -280 to 280, as said below
Outputs:
- normal: float32 [512, 512], P('row', 'grp')
- right_side: float32 [512], replicated
- diagonal: float32 [512], replicated
Inputs may be any that keep to these rules, and one draw needn't show every extreme that they name: `harmonic`: row 0 holds degrees from 2 to 280; row 1 holds orders whose magnitude is at most the column's degree; no two columns name the same pair; the pairs (280, 280) and (280, -280) are always present.
All inputs are finite; a program needn't handle non-finite values. No bound on the sum of `segment_start` on one device may be relied on, other than what follows from the above.
Results may differ from a plain program's by a relative error of at most 0.0041.
Values may be sent and summed in bfloat16 or wider, within the bound.
No kernel may reach another device: no remote copies, remote signals or barrier semaphores. Data moves between devices by JAX's collectives and lax.ppermute only.
A program may use at most 64 MiB of HBM per device.

v0:
```python
import math

import jax
import jax.numpy as jnp
from jax import lax
from jax.sharding import PartitionSpec as P


def passed_along(array, axis, by):
    length = lax.axis_size(axis)
    pairs = [(i, i + by) for i in range(length) if 0 <= i + by < length]
    return lax.ppermute(array, axis, pairs)


def design_rows(colatitude, longitude, harmonic):
    degree = harmonic[0].astype(jnp.float32)
    order_index = harmonic[1]
    polar_angle = colatitude[:, None] * degree[None, :]
    azimuth = longitude[:, None] * jnp.abs(order_index).astype(jnp.float32)[None, :]
    azimuth_wave = jnp.where(order_index[None, :] >= 0, jnp.cos(azimuth), jnp.sin(azimuth))
    radial = (jnp.cos(polar_angle) * azimuth_wave).astype(jnp.bfloat16)
    along = (jnp.sin(polar_angle) * azimuth_wave).astype(jnp.bfloat16)
    return (radial, along)


def on_device(colatitude, longitude, observed, filter_taps, segment_start, harmonic):
    rows_here = colatitude.shape[0]
    tap_count = filter_taps.shape[1]
    halo_rows = tap_count - 1
    panel_width = harmonic.shape[1]
    radial, along = design_rows(colatitude, longitude, harmonic)
    running = jnp.cumsum(segment_start)
    keep_tail = running[rows_here - halo_rows :] == running[rows_here - 1]
    keep_mask = keep_tail.astype(jnp.bfloat16)
    sent_rows = (
        radial[rows_here - halo_rows :] * keep_mask[:, None],
        along[rows_here - halo_rows :] * keep_mask[:, None],
        observed[:, rows_here - halo_rows :] * keep_mask[None, :],
    )
    halo_radial, halo_along, halo_signal = passed_along(
        (sent_rows[0], sent_rows[1], sent_rows[2]), "row", 1
    )
    labels = jnp.concatenate([jnp.zeros((halo_rows,), jnp.int32), running])
    windows = (
        jnp.concatenate([halo_radial, radial], axis=0),
        jnp.concatenate([halo_along, along], axis=0),
    )
    signal_window = jnp.concatenate([halo_signal, observed], axis=1)
    filtered = []
    filtered_signal = []
    for component in range(2):
        reversed_taps = filter_taps[component, ::-1]
        tap_seed = jnp.concatenate([reversed_taps, jnp.zeros((tap_count,), filter_taps.dtype)])
        tap_table = jnp.tile(tap_seed, tap_count)[: tap_count * (2 * tap_count - 1)].reshape(
            tap_count, 2 * tap_count - 1
        )
        pieces = []
        signal_pieces = []
        for block_index in range(rows_here // tap_count):
            block_low = block_index * tap_count
            in_label = labels[block_low : block_low + 2 * tap_count - 1]
            out_label = labels[block_low + halo_rows : block_low + halo_rows + tap_count]
            valid_mask = out_label[:, None] == in_label[None, :]
            matrix = jnp.where(valid_mask, tap_table, jnp.zeros((), tap_table.dtype))
            pieces.append(
                jnp.dot(
                    matrix,
                    windows[component][block_low : block_low + 2 * tap_count - 1],
                    preferred_element_type=jnp.float32,
                ).astype(jnp.bfloat16)
            )
            signal_pieces.append(
                jnp.dot(
                    matrix,
                    signal_window[component, block_low : block_low + 2 * tap_count - 1],
                    preferred_element_type=jnp.float32,
                ).astype(jnp.bfloat16)
            )
        filtered.append(jnp.concatenate(pieces, axis=0))
        filtered_signal.append(jnp.concatenate(signal_pieces, axis=0))
    rows_total = rows_here * lax.axis_size("grp") * lax.axis_size("row")
    row_scale = 1.0 / rows_total
    gram_scale = 1.0 / math.sqrt(rows_total)
    gram_sum = jnp.zeros(
        (lax.axis_size("row") * (panel_width // lax.axis_size("row")), panel_width), jnp.float32
    )
    for filtered_field in filtered:
        gram_sum = gram_sum + lax.dot_general(
            filtered_field,
            filtered_field,
            (((0,), (0,)), ((), ())),
            preferred_element_type=jnp.float32,
        )
    owned_tile = lax.psum_scatter(gram_sum * gram_scale, "row", scatter_dimension=0, tiled=True)
    normal = lax.psum_scatter(owned_tile, "grp", scatter_dimension=1, tiled=True)
    tile_rows = normal.shape[0]
    tile_cols = normal.shape[1]
    row_labels = lax.axis_index("row") * tile_rows + jnp.arange(tile_rows, dtype=jnp.int32)
    col_labels = lax.axis_index("grp") * tile_cols + jnp.arange(tile_cols, dtype=jnp.int32)
    normal = jnp.where(
        row_labels[:, None] == col_labels[None, :], jnp.zeros((), jnp.float32), normal
    )
    rhs_term = jnp.dot(filtered_signal[0], filtered[0], preferred_element_type=jnp.float32)
    rhs_term = rhs_term + jnp.dot(
        filtered_signal[1], filtered[1], preferred_element_type=jnp.float32
    )
    square_term = jnp.sum(jnp.square(filtered[0].astype(jnp.float32)), axis=0)
    square_term = square_term + jnp.sum(jnp.square(filtered[1].astype(jnp.float32)), axis=0)
    right_side, diagonal = lax.psum(
        (rhs_term * gram_scale, square_term * row_scale), ("grp", "row")
    )
    return (normal, right_side, diagonal)


def solution(mesh):
    placed = (
        P(("grp", "row")),
        P(("grp", "row")),
        P(None, ("grp", "row")),
        P(),
        P(("grp", "row")),
        P(),
    )
    return jax.shard_map(
        on_device,
        mesh=mesh,
        in_specs=placed,
        out_specs=(P("row", "grp"), P(), P()),
        check_vma=False,
    )
```

profile of v0, /device:TPU:1, one launch (start us, length us, event | category | flops | bytes accessed | tf_op | source)
XLA Modules:
  0.0 344.8 jit_solution(6376753127402647760)
XLA Ops:
  11.1 4.5 %collective-permute-start.2 = (bf16[2,255]{1,0:T(2,128)(2,1)}, bf16[2,255]{1,0:T(2,128)(2,1)}, u32[]{:S(2)}, u32[]{:S(2)}) collective-permute-start(bf16[2,255]{1,0:T(2,128)(2,1)} %slice_multiply_fusion.2), channel_id=1, source_target_pairs={{0,1},{1,2},{2,3},{3,4},{4,5},{5,6},{6,7},{7,8},{8,9},{9,10},{10,1... | collective-permute-start | bytes 3068 | tf_op jit(solution)/shard_map/ppermute | solution.py:12
  17.1 32.5 %fusion.3 = (bf16[2048,512]{1,0:T(8,128)(2,1)S(1)}, bf16[2048,512]{1,0:T(8,128)(2,1)S(1)}) fusion(f32[512]{0:T(512)S(1)} %bitcast.129, f32[2048]{0:T(1024)} %param.7, f32[512]{0:T(512)S(1)} %bitcast.128, f32[2048]{0:T(1024)} %param.6, pred[512]{0:T(512)(128)(4,1)S(1)} %compare_reduce_fusion), kind=kLoop, calls=%fused_computation.7 | loop fusion | flops 7340032 | bytes 4215296 | tf_op jit(solution)/shard_map/convert_element_type | solution.py:22
  49.6 1.4 copy-done.2
  51.9 1.9 collective-permute-start.1
  53.8 3.5 %collective-permute-start = (bf16[255,512]{1,0:T(8,128)(2,1)}, bf16[255,512]{1,0:T(8,128)(2,1)}, u32[]{:S(2)}, u32[]{:S(2)}) collective-permute-start(bf16[255,512]{1,0:T(8,128)(2,1)} %get-tuple-element.55), channel_id=1, source_target_pairs={{0,1},{1,2},{2,3},{3,4},{4,5},{5,6},{6,7},{7,8},{8,9},{9,10},{10,1... | collective-permute-start | bytes 783368 | tf_op jit(solution)/shard_map/ppermute | solution.py:12
  68.6 1.4 select_n.264
  70.8 1.4 select_n.254
  72.9 1.4 select_n.256
  75.1 1.4 select_n.258
  77.2 1.4 select_n.260
  79.4 1.4 select_n.262
  81.5 2.6 broadcast_select_fusion.8
  84.1 1.4 select_n.266
  85.7 1.4 select_n.280
  87.3 1.4 select_n.278
  91.3 2.2 select_n.274
  94.5 2.1 select_n.272
  100.8 1.4 reshape.322
  103.8 1.3 fusion.21
  114.5 2.3 fusion.5
  122.0 2.1 fusion.158
  125.5 107.7 %reduce-scatter.5.cloned.1.call-done = f32[16,512]{1,0:T(8,128)} async-done(((f32[512,512]{1,0:T(8,128)}), f32[16,512]{1,0:T(8,128)}) %reduce-scatter.5.cloned.1.call-update) | async-done | bytes 32784 | tf_op jit(solution)/shard_map/reduce_scatter | solution.py:94
  233.2 1.6 copy.9
  234.8 101.7 %all-reduce.3 = (f32[512]{0:T(512)}, f32[512]{0:T(512)}) all-reduce(f32[512]{0:T(512)S(1)} %add_multiply_fusion.1, f32[512]{0:T(512)S(1)} %add_multiply_fusion), channel_id=1, replica_groups=mesh['grp'=16,'row'=32] {'grp','row'}, use_global_device_ids=true, to_apply=%region_4.5 | all-reduce | flops 1024 | bytes 8192 | tf_op jit(solution)/shard_map/psum | solution.py:109
  (214 shorter events, 48.6 us)
Async XLA Ops:
  7.2 226.0 %reduce-scatter.5.cloned.1.call-start = ((), (), s32[]{:S(2)}) async-start(), calls=%async_computation.2 | async-start | bytes 1081344 | tf_op jit(solution)/shard_map/reduce_scatter | solution.py:94
  11.1 105.7 %collective-permute-start.2 = (bf16[2,255]{1,0:T(2,128)(2,1)}, bf16[2,255]{1,0:T(2,128)(2,1)}, u32[]{:S(2)}, u32[]{:S(2)}) collective-permute-start(bf16[2,255]{1,0:T(2,128)(2,1)} %slice_multiply_fusion.2), channel_id=1, source_target_pairs={{0,1},{1,2},{2,3},{3,4},{4,5},{5,6},{6,7},{7,8},{8,9},{9,10},{10,1... | collective-permute-start | bytes 3068 | tf_op jit(solution)/shard_map/ppermute | solution.py:12
  17.1 41.0 %copy-start.36 = (bf16[2,256]{1,0:T(2,128)(2,1)S(1)}, bf16[2,256]{1,0:T(2,128)(2,1)}, u32[]{:S(2)}) copy-start(bf16[2,256]{1,0:T(2,128)(2,1)} %param.9) | copy-start | bytes 3076
  51.9 57.5 %collective-permute-start.1 = (bf16[255,512]{1,0:T(8,128)(2,1)}, bf16[255,512]{1,0:T(8,128)(2,1)}, u32[]{:S(2)}, u32[]{:S(2)}) collective-permute-start(bf16[255,512]{1,0:T(8,128)(2,1)} %get-tuple-element.54), channel_id=1, source_target_pairs={{0,1},{1,2},{2,3},{3,4},{4,5},{5,6},{6,7},{7,8},{8,9},{9,10},{10,1... | collective-permute-start | bytes 783368 | tf_op jit(solution)/shard_map/ppermute | solution.py:12
  53.8 50.0 %collective-permute-start = (bf16[255,512]{1,0:T(8,128)(2,1)}, bf16[255,512]{1,0:T(8,128)(2,1)}, u32[]{:S(2)}, u32[]{:S(2)}) collective-permute-start(bf16[255,512]{1,0:T(8,128)(2,1)} %get-tuple-element.55), channel_id=1, source_target_pairs={{0,1},{1,2},{2,3},{3,4},{4,5},{5,6},{6,7},{7,8},{8,9},{9,10},{10,1... | collective-permute-start | bytes 783368 | tf_op jit(solution)/shard_map/ppermute | solution.py:12
  58.1 5.3 %copy-start.18 = (s32[511]{0:T(512)}, s32[511]{0:T(512)S(1)}, u32[]{:S(2)}) copy-start(s32[511]{0:T(512)S(1)} %get-tuple-element.46) | copy-start | bytes 6136
  58.1 5.3 %copy-start.20 = (s32[511]{0:T(512)}, s32[511]{0:T(512)S(1)}, u32[]{:S(2)}) copy-start(s32[511]{0:T(512)S(1)} %get-tuple-element.47) | copy-start | bytes 6136
  58.1 6.5 %copy-start.14 = (s32[511]{0:T(512)}, s32[511]{0:T(512)S(1)}, u32[]{:S(2)}) copy-start(s32[511]{0:T(512)S(1)} %get-tuple-element.44) | copy-start | bytes 6136
  58.1 6.5 %copy-start.16 = (s32[511]{0:T(512)}, s32[511]{0:T(512)S(1)}, u32[]{:S(2)}) copy-start(s32[511]{0:T(512)S(1)} %get-tuple-element.45) | copy-start | bytes 6136
  59.3 4.1 %copy-start.31 = (s32[256]{0:T(256)}, s32[256]{0:T(256)S(1)}, u32[]{:S(2)}) copy-start(s32[256]{0:T(256)S(1)} %get-tuple-element.38) | copy-start | bytes 3076
  59.3 4.1 %copy-start.33 = (s32[256]{0:T(256)}, s32[256]{0:T(256)S(1)}, u32[]{:S(2)}) copy-start(s32[256]{0:T(256)S(1)} %get-tuple-element.39) | copy-start | bytes 3076
  64.6 5.4 %copy-start.9 = (bf16[2,2048]{1,0:T(2,128)(2,1)S(1)}, bf16[2,2048]{1,0:T(2,128)(2,1)}, u32[]{:S(2)}) copy-start(bf16[2,2048]{1,0:T(2,128)(2,1)} %param.8) | copy-start | bytes 24580
  84.1 4.8 %copy-start.8 = (bf16[130816]{0:T(1024)(128)(2,1)S(1)}, bf16[130816]{0:T(1024)(128)(2,1)}, u32[]{:S(2)}) copy-start(bf16[130816]{0:T(1024)(128)(2,1)} %get-tuple-element.19) | copy-start | bytes 784900
  85.5 12.3 %copy-start.7 = (bf16[130816]{0:T(1024)(128)(2,1)S(1)}, bf16[130816]{0:T(1024)(128)(2,1)}, u32[]{:S(2)}) copy-start(bf16[130816]{0:T(1024)(128)(2,1)} %get-tuple-element.22) | copy-start | bytes 784900
  87.1 13.0 %copy-start.6 = (bf16[130816]{0:T(1024)(128)(2,1)S(1)}, bf16[130816]{0:T(1024)(128)(2,1)}, u32[]{:S(2)}) copy-start(bf16[130816]{0:T(1024)(128)(2,1)} %get-tuple-element.24) | copy-start | bytes 784900
  88.7 12.0 %copy-start.38 = (f32[1,256]{1,0:T(1,128)S(1)}, f32[1,256]{1,0:T(1,128)}, u32[]{:S(2)}) copy-start(f32[1,256]{1,0:T(1,128)} %fusion.109) | copy-start | bytes 3076
  90.1 12.1 %copy-start.37 = (f32[1,256]{1,0:T(1,128)S(1)}, f32[1,256]{1,0:T(1,128)}, u32[]{:S(2)}) copy-start(f32[1,256]{1,0:T(1,128)} %fusion.119) | copy-start | bytes 3076
  90.1 12.1 %copy-start.39 = (f32[1,256]{1,0:T(1,128)S(1)}, f32[1,256]{1,0:T(1,128)}, u32[]{:S(2)}) copy-start(f32[1,256]{1,0:T(1,128)} %fusion.117) | copy-start | bytes 3076
  90.1 12.1 %copy-start.40 = (f32[1,256]{1,0:T(1,128)S(1)}, f32[1,256]{1,0:T(1,128)}, u32[]{:S(2)}) copy-start(f32[1,256]{1,0:T(1,128)} %fusion.115) | copy-start | bytes 3076
  90.1 12.1 %copy-start.41 = (f32[1,256]{1,0:T(1,128)S(1)}, f32[1,256]{1,0:T(1,128)}, u32[]{:S(2)}) copy-start(f32[1,256]{1,0:T(1,128)} %fusion.113) | copy-start | bytes 3076
  90.1 12.1 %copy-start.42 = (f32[1,256]{1,0:T(1,128)S(1)}, f32[1,256]{1,0:T(1,128)}, u32[]{:S(2)}) copy-start(f32[1,256]{1,0:T(1,128)} %fusion.111) | copy-start | bytes 3076
  90.1 12.2 %copy-start.5 = (bf16[130816]{0:T(1024)(128)(2,1)S(1)}, bf16[130816]{0:T(1024)(128)(2,1)}, u32[]{:S(2)}) copy-start(bf16[130816]{0:T(1024)(128)(2,1)} %get-tuple-element.16) | copy-start | bytes 784900
  91.3 11.5 %copy-start.4 = (bf16[130816]{0:T(1024)(128)(2,1)S(1)}, bf16[130816]{0:T(1024)(128)(2,1)}, u32[]{:S(2)}) copy-start(bf16[130816]{0:T(1024)(128)(2,1)} %get-tuple-element.15) | copy-start | bytes 784900
  116.8 219.7 %reduce-scatter.7.cloned.1.call-start = ((), (), s32[]{:S(2)}) async-start(), calls=%async_computation.3 | async-start | bytes 278528
  (24 other events, 39.5 us)
Sparse Core Ops, SparseCore 0:
  116.9 116.2 reduce-scatter.4
  236.0 74.4 reduce-scatter.6
where the time goes:
time: 346 us; the launch traced here: 345 us
  waiting for transfers between devices  108 us (31%)
  blocking collectives  102 us (29%)
  other arithmetic  45.4 us (13%)
  local copies, waits for them, and re-layouts  39.5 us (11%)
  matrix products  25.5 us (7%)
  between operations  15 us (4%)
  starting transfers between devices  9.98 us (3%)
    reduce_scatter x1, waiting for transfers between devices, on_device(): lax.psum_scatter(gram_sum * gram_scale, 'row', scatter_dimension=0, tiled...  108 us
    psum x1, blocking collectives, on_device(): lax.psum((rhs_term * gram_scale, square_term * row_scale), ('grp', 'row'))  102 us
    convert_element_type x1, other arithmetic, design_rows(): along = (jnp.sin(polar_angle) * azimuth_wave).astype(jnp.bfloat16)  32.5 us
    select_n x16, local copies, waits for them, and re-layouts, on_device(): matrix = jnp.where(valid_mask, tap_table, jnp.zeros((), tap_table.dtype))  20.5 us
    dot_general x16, matrix products, on_device(): jnp.dot(matrix, signal_window[component, block_low:block_low + 2 * tap_co...  11.5 us
    ppermute x3, starting transfers between devices, passed_along(): return lax.ppermute(array, axis, pairs)  9.9 us
    unnamed x106, local copies, waits for them, and re-layouts  8.95 us
    dot_general x16, matrix products, on_device(): jnp.dot(matrix, windows[component][block_low:block_low + 2 * tap_count -...  8 us
  transfers between devices with their start and end apart: 5, of which 1 were waited for; matrix products, arithmetic and copies ran while one was open for 29% of the time, Pallas kernels for 0%

commit v1 on v0

v1 whole, which is shorter than its diff:
```python
import functools
import math

import jax
import jax.numpy as jnp
from jax import lax
from jax.experimental import pallas as pl
from jax.experimental.pallas import tpu as pltpu
from jax.sharding import Mesh, PartitionSpec as P

F32 = jnp.float32
BF16 = jnp.bfloat16
LANES = 128
TAPS = 256
SIN_COEFFS = (3.141592639, -5.167709953, 2.550074404, -0.5982681334, 0.07760505745)
COS_COEFFS = (0.9999999504, -4.934792377, 4.058400535, -1.331796279, 0.2195071918)
TWO_PI_PARTS = (6.28125, 0.0019340515136718750, 1.2556659146854654e-06)
HALF_UP = 1.5 * 2.0**23


def horner(coeffs, z):
    total = z * coeffs[-1] + coeffs[-2]
    for coeff in coeffs[-3::-1]:
        total = total * z + coeff
    return total


def nearest(value):
    return (value + HALF_UP) - HALF_UP


def turns_of(angle):
    coarse = nearest(angle * (65536.0 / (2.0 * math.pi))) * (1.0 / 65536.0)
    rest = angle
    for part in TWO_PI_PARTS:
        rest = rest - coarse * part
    return coarse, rest * (1.0 / (2.0 * math.pi))


def dot_nt(a, b):
    return lax.dot_general(a, b, (((1,), (1,)), ((), ())), preferred_element_type=F32)


def dot_nn(a, b):
    return lax.dot_general(a, b, (((1,), (0,)), ((), ())), preferred_element_type=F32)


def iota(shape, axis):
    return lax.broadcasted_iota(jnp.int32, shape, axis)


def gram_kernel(
    colat_ref,
    lon_ref,
    obs_ref,
    start_ref,
    halo_ref,
    harmonic_ref,
    taps_ref,
    out_ref,
    design,
    filtered,
    matrices,
    columns,
    turns,
    starts,
    gram,
    *,
    panel,
    blocks,
    row_scale,
    gram_scale,
):
    own_rows = blocks * 2
    all_rows = own_rows + 2

    wide = harmonic_ref[...].astype(F32)
    tall = jnp.transpose(jnp.concatenate([wide, jnp.zeros((6, panel), F32)], axis=0))
    for zl in range(4):
        for y in range(4):
            part = tall[zl * 128 + y * 32 : zl * 128 + y * 32 + 32, :]
            low = y * 128 + zl * 32
            degree = jnp.broadcast_to(part[:, 0:1], (32, LANES))
            order = jnp.broadcast_to(part[:, 1:2], (32, LANES))
            columns[0, low : low + 32, :] = degree
            columns[1, low : low + 32, :] = jnp.abs(order)
            columns[2, low : low + 32, :] = jnp.where(order < 0.0, 0.25, 0.0)

    for slot, (own, halo_low) in enumerate(((colat_ref, 0), (lon_ref, 2))):
        coarse, fine = turns_of(halo_ref[halo_low : halo_low + 2, :])
        turns[2 * slot, 0:2, :] = coarse
        turns[2 * slot + 1, 0:2, :] = fine
        coarse, fine = turns_of(own[...])
        turns[2 * slot, 2 : 2 + own_rows, :] = coarse
        turns[2 * slot + 1, 2 : 2 + own_rows, :] = fine

    starts[...] = jnp.zeros_like(starts)
    starts[0:2, :] = halo_ref[8:10, :]
    starts[2 : 2 + own_rows, :] = start_ref[...].astype(F32)
    flags = starts[...].astype(BF16)
    square = (LANES, LANES)
    low_tri = (iota(square, 0) >= iota(square, 1)).astype(BF16)
    up_tri = (iota(square, 0) <= iota(square, 1)).astype(BF16)
    low_strict = (iota(square, 0) > iota(square, 1)).astype(BF16)
    up_strict = (iota(square, 0) < iota(square, 1)).astype(BF16)
    ones = jnp.ones(square, BF16)
    lonely = 1.0 - halo_ref[10:11, :]
    label_row = dot_nn(flags, up_tri) + dot_nn(dot_nn(low_strict, flags).astype(BF16), ones)
    label_row = label_row + jnp.where(iota(square, 0) >= 2, lonely, 0.0)
    label_col = dot_nt(low_tri, flags) + dot_nn(dot_nt(ones, flags).astype(BF16), up_strict)
    label_col = label_col + jnp.where(iota(square, 1) >= 2, lonely, 0.0)

    toeplitz = []
    for component in range(2):
        padded = jnp.concatenate(
            [taps_ref[component : component + 1, :].astype(F32), jnp.zeros((1, TAPS), F32)], axis=1
        )
        spread = jnp.broadcast_to(padded, (LANES, 2 * TAPS))
        rolled = pltpu.roll(spread, 0, 1, stride=1, stride_axis=0)
        toeplitz.append([rolled[:, d * LANES : (d + 1) * LANES] for d in range(3)])
    for block in range(blocks):
        for sb in range(4):
            source = 2 * block + sb
            left = jnp.broadcast_to(label_col[:, source : source + 1], square)
            for tb in range(2):
                d = tb - sb + 2
                place = (slice(sb * LANES, (sb + 1) * LANES), slice(tb * LANES, (tb + 1) * LANES))
                if 0 <= d <= 2:
                    target = 2 * block + 2 + tb
                    same = left == label_row[target : target + 1, :]
                    for component in range(2):
                        kept = jnp.where(same, toeplitz[component][d], 0.0)
                        matrices[block, component, place[0], place[1]] = kept.astype(BF16)
                else:
                    for component in range(2):
                        matrices[block, component, place[0], place[1]] = jnp.zeros(square, BF16)

    def some_columns(step, carry):
        low = pl.multiple_of(step * 16, 16)
        degree = columns[0, pl.ds(low, 16), :]
        order = columns[1, pl.ds(low, 16), :]
        phase = columns[2, pl.ds(low, 16), :]
        for chunk in range(all_rows):
            row = slice(chunk, chunk + 1)
            lane = slice(chunk * LANES, (chunk + 1) * LANES)
            polar = degree * turns[0, row, :]
            polar = (polar - nearest(polar)) + degree * turns[1, row, :]
            z = polar * polar
            half_sin = polar * horner(SIN_COEFFS, z)
            half_cos = horner(COS_COEFFS, z)
            twice = half_sin + half_sin
            cos_polar = 1.0 - twice * half_sin
            sin_polar = twice * half_cos
            azimuth = order * turns[2, row, :] - phase
            azimuth = (azimuth - nearest(azimuth)) + order * turns[3, row, :]
            half = azimuth * horner(SIN_COEFFS, azimuth * azimuth)
            wave = 1.0 - (half + half) * half
            design[0, pl.ds(low, 16), lane] = (cos_polar * wave).astype(BF16)
            design[1, pl.ds(low, 16), lane] = (sin_polar * wave).astype(BF16)
        return carry

    lax.fori_loop(0, panel // 16, some_columns, 0)

    for component in range(2):
        halo = jnp.concatenate(
            [halo_ref[4 + 2 * component : 5 + 2 * component, :], halo_ref[5 + 2 * component : 6 + 2 * component, :]],
            axis=1,
        )
        design[component, panel : panel + 16, 0:TAPS] = jnp.where(
            iota((16, TAPS), 0) == 0, halo, 0.0
        ).astype(BF16)
        span = own_rows * LANES
        own = obs_ref[component : component + 1, :].astype(F32)
        design[component, panel : panel + 16, TAPS : TAPS + span] = jnp.where(
            iota((16, span), 0) == 0, own, 0.0
        ).astype(BF16)

    for component in range(2):
        for block in range(blocks):
            window = design[component, :, block * TAPS : block * TAPS + 2 * TAPS]
            low = (component * blocks + block) * TAPS
            filtered[:, low : low + TAPS] = dot_nn(window, matrices[block, component]).astype(BF16)

    gram[...] = dot_nt(filtered[...], filtered[0:panel, :])

    eye = iota(square, 0) == iota(square, 1)
    rhs = [gram[panel : panel + 1, y * LANES : (y + 1) * LANES] * gram_scale for y in range(4)]
    diagonal = [
        jnp.sum(
            jnp.where(eye, gram[y * LANES : (y + 1) * LANES, y * LANES : (y + 1) * LANES], 0.0),
            axis=0,
            keepdims=True,
        )
        * row_scale
        for y in range(4)
    ]
    small = jnp.concatenate(rhs + diagonal + [jnp.zeros((8, LANES), F32)], axis=0).astype(BF16)
    for y in range(4):
        for x in range(4):
            for core in range(2):
                peer = y * 8 + x * 2 + core
                for zh in range(4):
                    low = x * 128 + zh * 32 + core * 16
                    out_ref[peer, zh * 16 : zh * 16 + 16, :] = (
                        gram[low : low + 16, y * LANES : (y + 1) * LANES] * gram_scale
                    ).astype(BF16)
                out_ref[peer, 64:80, :] = small


def middle_kernel(in_ref, out_ref):
    total = in_ref[0].astype(F32)
    for peer in range(1, in_ref.shape[0]):
        total = total + in_ref[peer].astype(F32)
    small = total[64:72, :]
    for zl in range(4):
        for zh in range(4):
            peer = zl * 4 + zh
            for b in range(4):
                rows = total[zh * 16 + 4 * b : zh * 16 + 4 * b + 4, zl * 32 : zl * 32 + 32]
                out_ref[peer, 0:4, b * 32 : b * 32 + 32] = rows
            out_ref[peer, 8:16, :] = small


def last_kernel(row_ref, in_ref, normal_ref, rhs_ref, diagonal_ref):
    total = in_ref[0]
    for peer in range(1, in_ref.shape[0]):
        total = total + in_ref[peer]
    for b in range(4):
        normal_ref[4 * b : 4 * b + 4, :] = total[0:4, b * 32 : b * 32 + 32]
    rows, cols = normal_ref.shape
    row_label = row_ref[0] + iota((rows, cols), 0)
    col_label = row_ref[1] + iota((rows, cols), 1)
    normal_ref[...] = jnp.where(row_label == col_label, 0.0, normal_ref[...])
    for out_ref, low in ((rhs_ref, 8), (diagonal_ref, 12)):
        for zl in range(4):
            for y in range(4):
                out_ref[0:1, zl * 128 + y * 32 : zl * 128 + y * 32 + 32] = total[
                    low + y : low + y + 1, zl * 32 : zl * 32 + 32
                ]


def on_device(colatitude, longitude, observed, filter_taps, segment_start, harmonic):
    rows_here = colatitude.shape[0]
    panel = harmonic.shape[1]
    blocks = rows_here // TAPS
    rows_total = rows_here * 512
    tail = rows_here - TAPS
    pieces = [
        colatitude[tail:],
        longitude[tail:],
        observed[0, tail:].astype(F32),
        observed[1, tail:].astype(F32),
        segment_start[tail:].astype(F32),
        jnp.ones((768,), F32),
    ]
    packed = jnp.concatenate(pieces)
    length = 32
    halo = lax.ppermute(packed, ("zh", "x", "core"), [(i, i + 1) for i in range(length - 1)])

    vmem = pl.BlockSpec(memory_space=pltpu.VMEM)
    kernel = functools.partial(
        gram_kernel,
        panel=panel,
        blocks=blocks,
        row_scale=1.0 / rows_total,
        gram_scale=1.0 / math.sqrt(rows_total),
    )
    payload = pl.pallas_call(
        kernel,
        name="gram_of_arc_part",
        out_shape=jax.ShapeDtypeStruct((32, 80, LANES), BF16),
        in_specs=[vmem] * 7,
        out_specs=vmem,
        scratch_shapes=[
            pltpu.VMEM((2, panel + 16, rows_here + TAPS), BF16),
            pltpu.VMEM((panel + 16, 2 * rows_here), BF16),
            pltpu.VMEM((blocks, 2, 2 * TAPS, TAPS), BF16),
            pltpu.VMEM((3, panel, LANES), F32),
            pltpu.VMEM((4, 24, LANES), F32),
            pltpu.VMEM((LANES, LANES), F32),
            pltpu.VMEM((panel + 16, panel), F32),
        ],
        compiler_params=pltpu.CompilerParams(vmem_limit_bytes=48 * 1024 * 1024),
    )(
        colatitude.reshape(-1, LANES),
        longitude.reshape(-1, LANES),
        observed,
        segment_start.reshape(-1, LANES),
        halo.reshape(-1, LANES),
        harmonic,
        filter_taps,
    )
    arrived = lax.all_to_all(payload, ("y", "x", "core"), 0, 0)
    packed_sums = pl.pallas_call(
        middle_kernel,
        name="sum_over_plane",
        out_shape=jax.ShapeDtypeStruct((16, 16, LANES), F32),
        in_specs=[vmem],
        out_specs=vmem,
    )(arrived)
    gathered = lax.all_to_all(packed_sums, ("zl", "zh"), 0, 0)
    row_low = (lax.axis_index("zh") * 8 + lax.axis_index("x") * 2 + lax.axis_index("core")) * 16
    col_low = (lax.axis_index("zl") * 4 + lax.axis_index("y")) * 32
    corner = jnp.stack([row_low, col_low]).astype(jnp.int32)
    normal, right_side, diagonal = pl.pallas_call(
        last_kernel,
        name="sum_over_z",
        out_shape=(
            jax.ShapeDtypeStruct((16, 32), F32),
            jax.ShapeDtypeStruct((1, panel), F32),
            jax.ShapeDtypeStruct((1, panel), F32),
        ),
        in_specs=[pl.BlockSpec(memory_space=pltpu.SMEM), vmem],
        out_specs=(vmem, vmem, vmem),
    )(corner, gathered)
    return normal, right_side.reshape(panel), diagonal.reshape(panel)


def solution(mesh):
    fine = Mesh(mesh.devices.reshape(4, 4, 4, 4, 2), ("zl", "y", "zh", "x", "core"))
    everywhere = ("zl", "y", "zh", "x", "core")
    return jax.shard_map(
        on_device,
        mesh=fine,
        in_specs=(P(everywhere), P(everywhere), P(None, everywhere), P(), P(everywhere), P()),
        out_specs=(P(("zh", "x", "core"), ("zl", "y")), P(), P()),
        check_vma=False,
    )
```

time: 346 us -> 81.9 us (0.24)
  the two profiles are of different devices: /device:TPU:1 before, /device:TPU:32 now
where the time goes in v1:
time: 81.9 us; the launch traced here: 81.5 us
  blocking collectives  27 us (33%)
  Pallas kernels  17.5 us (21%)
  starting transfers between devices  16.2 us (20%)
  waiting for transfers between devices  15.1 us (18%)
  local copies, waits for them, and re-layouts  3.41 us (4%)
  other arithmetic  1.43 us (2%)
    all_to_all x1, blocking collectives, on_device(): arrived = lax.all_to_all(payload, ('y', 'x', 'core'), 0, 0)  27 us
    all_to_all x1, starting transfers between devices, on_device(): gathered = lax.all_to_all(packed_sums, ('zl', 'zh'), 0, 0)  14.5 us
    all_to_all x1, waiting for transfers between devices, on_device(): gathered = lax.all_to_all(packed_sums, ('zl', 'zh'), 0, 0)  14.3 us
    pallas_call x1, Pallas kernels, on_device(): pl.pallas_call(kernel, name='gram_of_arc_part', out_shape=jax.ShapeDtypeS...  14 us
    unnamed x18, local copies, waits for them, and re-layouts  3.41 us
    pallas_call x1, Pallas kernels, on_device(): pl.pallas_call(middle_kernel, name='sum_over_plane', out_shape=jax.ShapeD...  1.89 us
    ppermute x1, starting transfers between devices, on_device(): lax.ppermute(packed, ('zh', 'x', 'core'), [(i, i + 1) for i in range(leng...  1.74 us
  transfers between devices with their start and end apart: 2, of which 2 were waited for; matrix products, arithmetic and copies ran while one was open for 1% of the time, Pallas kernels for 0%

profile of v1, /device:TPU:32, one launch (start us, length us, event | category | flops | bytes accessed | tf_op | source)
XLA Modules:
  0.0 81.5 jit_solution(7445671087215284961)
XLA Ops:
  0.6 0.0 copy-start.3
  0.7 0.8 slice_convert_fusion
  1.4 0.7 constant_dynamic-update-slice_fusion.5
  2.1 0.7 constant_dynamic-update-slice_fusion.4
  2.8 0.0 copy-start.2
  2.8 0.0 copy-start.1
  2.8 0.0 copy-start
  2.8 0.0 copy-done.3
  2.9 1.7 %collective-permute-start = (f32[2048]{0:T(1024)S(1)}, f32[2048]{0:T(1024)S(1)}, u32[]{:S(2)}, u32[]{:S(2)}) collective-permute-start(f32[2048]{0:T(1024)S(1)} %constant_dynamic-update-slice_fusion), channel_id=1, source_target_pairs={{0,1},{1,2},{2,3},{3,4},{4,5},{5,6},{6,7},{7,8},{8,9},{9,10},{10,1... | collective-permute-start | bytes 24584 | tf_op jit(solution)/shard_map/ppermute | solution.py:258
  4.6 0.8 collective-permute-done
  5.4 0.0 copy-start.5
  5.4 0.0 copy-done.2
  5.4 0.0 copy-done.1
  5.4 0.0 copy-done
  5.5 0.7 copy-done.5
  6.1 0.7 copy-done.4
  6.8 14.0 %gram_of_arc_part.1 = bf16[32,80,128]{2,1,0:T(8,128)(2,1)S(1)} custom-call(f32[16,128]{1,0:T(8,128)S(1)} %bitcast.10, f32[16,128]{1,0:T(8,128)S(1)} %bitcast.11, bf16[2,2048]{1,0:T(2,128)(2,1)S(1)} %copy-done, s32[16,128]{1,0:T(8,128)S(1)} %bitcast.12, f32[16,128]{1,0:T(8,128)S(1)} %bitcast.13, s32[2,512]{1,0:T(2,128)S(1)} %copy-done.4, ...), custom_call_target="tpu_custom_call" | custom-call | tf_op jit(solution)/shard_map/gram_of_arc_part/pallas_call | solution.py:268
  20.9 27.0 %all_to_all.10.in_ref = bf16[32,80,128]{2,1,0:T(8,128)(2,1)} all-to-all(bf16[32,80,128]{2,1,0:T(8,128)(2,1)S(1)} %gram_of_arc_part.1), channel_id=1, replica_groups=mesh['zl'=4,'y'=4,'zh'=4,'x'=4,'core'=2] {'y','x','core'}, dimensions={0} | all-to-all | bytes 1310720 | tf_op jit(solution)/shard_map/all_to_all | solution.py:293
  47.9 1.9 %sum_over_plane.1 = f32[16,16,128]{2,1,0:T(8,128)} custom-call(bf16[32,80,128]{2,1,0:T(8,128)(2,1)} %all_to_all.10.in_ref), custom_call_target="tpu_custom_call" | custom-call | tf_op jit(solution)/shard_map/sum_over_plane/pallas_call | solution.py:294
  49.8 14.5 %all-to-all-start.1 = ((f32[16,16,128]{2,1,0:T(8,128)}), f32[16,16,128]{2,1,0:T(8,128)S(1)}, u32[]{:S(2)}, u32[]{:S(2)}) async-start(f32[16,16,128]{2,1,0:T(8,128)} %sum_over_plane.1), calls=%async_computation.1 | async-start | bytes 262144 | tf_op jit(solution)/shard_map/all_to_all | solution.py:301
  64.3 0.7 pad_add_fusion.row_ref
  64.9 14.3 %all-to-all-done.1.in_ref = f32[16,16,128]{2,1,0:T(8,128)S(1)} async-done(((f32[16,16,128]{2,1,0:T(8,128)}), f32[16,16,128]{2,1,0:T(8,128)S(1)}, u32[]{:S(2)}, u32[]{:S(2)}) %all-to-all-start.1) | async-done | bytes 131104 | tf_op jit(solution)/shard_map/all_to_all | solution.py:301
  79.2 0.6 copy-done.6
  79.8 1.6 %sum_over_z.1 = (f32[16,32]{1,0:T(8,128)}, f32[1,512]{1,0:T(1,128)}, f32[1,512]{1,0:T(1,128)}) custom-call(s32[2]{0:T(128)} %pad_add_fusion.row_ref, f32[16,16,128]{2,1,0:T(8,128)} %copy-done.6), custom_call_target="tpu_custom_call" | custom-call | tf_op jit(solution)/shard_map/sum_over_z/pallas_call | solution.py:305
  (7 shorter events, 0.0 us)
Async XLA Ops:
  0.6 2.2 %copy-start.3 = (s32[2048]{0:T(1024)S(1)}, s32[2048]{0:T(1024)}, u32[]{:S(2)}) copy-start(s32[2048]{0:T(1024)} %param.10) | copy-start | bytes 24580
  2.8 2.6 %copy-start.2 = (f32[2048]{0:T(1024)S(1)}, f32[2048]{0:T(1024)}, u32[]{:S(2)}) copy-start(f32[2048]{0:T(1024)} %param.7) | copy-start | bytes 24580
  2.8 2.6 %copy-start.1 = (f32[2048]{0:T(1024)S(1)}, f32[2048]{0:T(1024)}, u32[]{:S(2)}) copy-start(f32[2048]{0:T(1024)} %param.6) | copy-start | bytes 24580
  2.8 2.6 %copy-start = (bf16[2,2048]{1,0:T(2,128)(2,1)S(1)}, bf16[2,2048]{1,0:T(2,128)(2,1)}, u32[]{:S(2)}) copy-start(bf16[2,2048]{1,0:T(2,128)(2,1)} %obs_ref.1) | copy-start | bytes 24580
  2.9 2.6 %collective-permute-start = (f32[2048]{0:T(1024)S(1)}, f32[2048]{0:T(1024)S(1)}, u32[]{:S(2)}, u32[]{:S(2)}) collective-permute-start(f32[2048]{0:T(1024)S(1)} %constant_dynamic-update-slice_fusion), channel_id=1, source_target_pairs={{0,1},{1,2},{2,3},{3,4},{4,5},{5,6},{6,7},{7,8},{8,9},{9,10},{10,1... | collective-permute-start | bytes 24584 | tf_op jit(solution)/shard_map/ppermute | solution.py:258
  5.4 0.7 copy-start.5
  6.1 0.7 copy-start.4
  49.8 29.5 %all-to-all-start.1 = ((f32[16,16,128]{2,1,0:T(8,128)}), f32[16,16,128]{2,1,0:T(8,128)S(1)}, u32[]{:S(2)}, u32[]{:S(2)}) async-start(f32[16,16,128]{2,1,0:T(8,128)} %sum_over_plane.1), calls=%async_computation.1 | async-start | bytes 262144 | tf_op jit(solution)/shard_map/all_to_all | solution.py:301
  79.2 0.6 copy-start.6

commit v2 on v1

v2 whole, which is shorter than its diff:
```python
import functools
import math

import jax
import jax.numpy as jnp
from jax import lax
from jax.experimental import pallas as pl
from jax.experimental.pallas import tpu as pltpu
from jax.sharding import Mesh, PartitionSpec as P

F32 = jnp.float32
BF16 = jnp.bfloat16
LANES = 128
TAPS = 256
SIN_COEFFS = (3.141592639, -5.167709953, 2.550074404, -0.5982681334, 0.07760505745)
COS_COEFFS = (0.9999999504, -4.934792377, 4.058400535, -1.331796279, 0.2195071918)
TWO_PI_PARTS = (6.28125, 0.0019340515136718750, 1.2556659146854654e-06)
HALF_UP = 1.5 * 2.0**23


def horner(coeffs, z):
    total = z * coeffs[-1] + coeffs[-2]
    for coeff in coeffs[-3::-1]:
        total = total * z + coeff
    return total


def nearest(value):
    return (value + HALF_UP) - HALF_UP


def turns_of(angle):
    coarse = nearest(angle * (65536.0 / (2.0 * math.pi))) * (1.0 / 65536.0)
    rest = angle
    for part in TWO_PI_PARTS:
        rest = rest - coarse * part
    return coarse, rest * (1.0 / (2.0 * math.pi))


def dot_nt(a, b):
    return lax.dot_general(a, b, (((1,), (1,)), ((), ())), preferred_element_type=F32)


def dot_nn(a, b):
    return lax.dot_general(a, b, (((1,), (0,)), ((), ())), preferred_element_type=F32)


def iota(shape, axis):
    return lax.broadcasted_iota(jnp.int32, shape, axis)


def spread_turns(turns, angle, slot, low):
    coarse, fine = turns_of(angle)
    turns[2 * slot, low : low + angle.shape[0], :] = coarse
    turns[2 * slot + 1, low : low + angle.shape[0], :] = fine


def fill_design(design, columns, turns, chunks):
    def some_columns(step, carry):
        low = pl.multiple_of(step * 16, 16)
        degree = columns[0, pl.ds(low, 16), :]
        order = columns[1, pl.ds(low, 16), :]
        phase = columns[2, pl.ds(low, 16), :]
        for chunk in range(chunks):
            row = slice(chunk, chunk + 1)
            lane = slice(chunk * LANES, (chunk + 1) * LANES)
            polar = degree * turns[0, row, :]
            polar = (polar - nearest(polar)) + degree * turns[1, row, :]
            z = polar * polar
            half_sin = polar * horner(SIN_COEFFS, z)
            half_cos = horner(COS_COEFFS, z)
            twice = half_sin + half_sin
            cos_polar = 1.0 - twice * half_sin
            sin_polar = twice * half_cos
            azimuth = order * turns[2, row, :] - phase
            azimuth = (azimuth - nearest(azimuth)) + order * turns[3, row, :]
            half = azimuth * horner(SIN_COEFFS, azimuth * azimuth)
            wave = 1.0 - (half + half) * half
            design[0, pl.ds(low, 16), lane] = (cos_polar * wave).astype(BF16)
            design[1, pl.ds(low, 16), lane] = (sin_polar * wave).astype(BF16)
        return carry

    lax.fori_loop(0, columns.shape[1] // 16, some_columns, 0)


def fill_signal(design, component, panel, values):
    span = values.shape[1]
    design[component, panel : panel + 16, 0:span] = jnp.where(
        iota((16, span), 0) == 0, values, 0.0
    ).astype(BF16)


def labels_of(flags):
    square = (LANES, LANES)
    low_tri = (iota(square, 0) >= iota(square, 1)).astype(BF16)
    up_tri = (iota(square, 0) <= iota(square, 1)).astype(BF16)
    low_strict = (iota(square, 0) > iota(square, 1)).astype(BF16)
    up_strict = (iota(square, 0) < iota(square, 1)).astype(BF16)
    ones = jnp.ones(square, BF16)
    by_lane = dot_nn(flags, up_tri) + dot_nn(dot_nn(low_strict, flags).astype(BF16), ones)
    by_sublane = dot_nt(low_tri, flags) + dot_nn(dot_nt(ones, flags).astype(BF16), up_strict)
    return by_lane, by_sublane


def fill_matrices(matrices, block, first_row, by_lane, by_sublane, toeplitz):
    square = (LANES, LANES)
    for sb in range(4):
        left = jnp.broadcast_to(by_sublane[:, first_row + sb : first_row + sb + 1], square)
        for tb in range(2):
            d = tb - sb + 2
            place = (slice(sb * LANES, (sb + 1) * LANES), slice(tb * LANES, (tb + 1) * LANES))
            if 0 <= d <= 2:
                same = left == by_lane[first_row + 2 + tb : first_row + 3 + tb, :]
                for component in range(2):
                    kept = jnp.where(same, toeplitz(component, d), 0.0)
                    matrices[block, component, place[0], place[1]] = kept.astype(BF16)
            else:
                for component in range(2):
                    matrices[block, component, place[0], place[1]] = jnp.zeros(square, BF16)


def own_kernel(
    colat_ref,
    lon_ref,
    obs_ref,
    start_ref,
    harmonic_ref,
    taps_ref,
    gram_ref,
    head_ref,
    columns_ref,
    toeplitz_ref,
    design,
    filtered,
    matrices,
    turns,
    starts,
):
    rows, _ = colat_ref.shape
    panel = harmonic_ref.shape[1]
    blocks = rows // 2

    wide = harmonic_ref[...].astype(F32)
    tall = jnp.transpose(jnp.concatenate([wide, jnp.zeros((6, panel), F32)], axis=0))
    for zl in range(4):
        for y in range(4):
            part = tall[zl * 128 + y * 32 : zl * 128 + y * 32 + 32, :]
            low = y * 128 + zl * 32
            degree = jnp.broadcast_to(part[:, 0:1], (32, LANES))
            order = jnp.broadcast_to(part[:, 1:2], (32, LANES))
            columns_ref[0, low : low + 32, :] = degree
            columns_ref[1, low : low + 32, :] = jnp.abs(order)
            columns_ref[2, low : low + 32, :] = jnp.where(order < 0.0, 0.25, 0.0)

    spread_turns(turns, colat_ref[...], 0, 0)
    spread_turns(turns, lon_ref[...], 1, 0)

    starts[...] = jnp.zeros_like(starts)
    starts[0:rows, :] = start_ref[...].astype(F32)
    by_lane, by_sublane = labels_of(starts[...].astype(BF16))

    for component in range(2):
        padded = jnp.concatenate(
            [taps_ref[component : component + 1, :].astype(F32), jnp.zeros((1, TAPS), F32)], axis=1
        )
        spread = jnp.broadcast_to(padded, (LANES, 2 * TAPS))
        rolled = pltpu.roll(spread, 0, 1, stride=1, stride_axis=0)
        for d in range(3):
            toeplitz_ref[component, d] = rolled[:, d * LANES : (d + 1) * LANES]
    for block in range(blocks - 1):
        fill_matrices(
            matrices, block, 2 * block, by_lane, by_sublane, lambda c, d: toeplitz_ref[c, d]
        )

    fill_design(design, columns_ref, turns, rows)
    for component in range(2):
        fill_signal(design, component, panel, obs_ref[component : component + 1, :].astype(F32))
        head_ref[component] = design[component, :, 0:TAPS]

    for component in range(2):
        for block in range(blocks - 1):
            window = design[component, :, block * TAPS : block * TAPS + 2 * TAPS]
            low = (component * (blocks - 1) + block) * TAPS
            filtered[:, low : low + TAPS] = dot_nn(window, matrices[block, component]).astype(BF16)
    gram_ref[...] = dot_nt(filtered[...], filtered[0:panel, :])


def edge_kernel(
    halo_ref,
    start_ref,
    before_ref,
    head_ref,
    columns_ref,
    toeplitz_ref,
    out_ref,
    design,
    filtered,
    matrices,
    turns,
    starts,
    gram,
    *,
    row_scale,
    gram_scale,
):
    panel = columns_ref.shape[1]
    spread_turns(turns, halo_ref[0:2, :], 0, 0)
    spread_turns(turns, halo_ref[2:4, :], 1, 0)

    square = (LANES, LANES)
    starts[...] = jnp.zeros_like(starts)
    starts[0:2, :] = halo_ref[8:10, :]
    starts[2:4, :] = start_ref[0:2, :].astype(F32)
    by_lane, by_sublane = labels_of(starts[...].astype(BF16))
    lonely = 1.0 - halo_ref[10:11, :]
    by_lane = by_lane + jnp.where(iota(square, 0) >= 2, lonely, 0.0)
    by_sublane = by_sublane + jnp.where(iota(square, 1) >= 2, lonely, 0.0)
    fill_matrices(matrices, 0, 0, by_lane, by_sublane, lambda c, d: toeplitz_ref[c, d])

    fill_design(design, columns_ref, turns, 2)
    for component in range(2):
        low = 4 + 2 * component
        halo = jnp.concatenate([halo_ref[low : low + 1, :], halo_ref[low + 1 : low + 2, :]], axis=1)
        fill_signal(design, component, panel, halo)
        sums = dot_nn(design[component], matrices[0, component, 0:TAPS, :]) + dot_nn(
            head_ref[component], matrices[0, component, TAPS : 2 * TAPS, :]
        )
        filtered[:, component * TAPS : (component + 1) * TAPS] = sums.astype(BF16)

    gram[...] = before_ref[...] + dot_nt(filtered[...], filtered[0:panel, :])

    eye = iota(square, 0) == iota(square, 1)
    rhs = [gram[panel : panel + 1, y * LANES : (y + 1) * LANES] * gram_scale for y in range(4)]
    diagonal = [
        jnp.sum(
            jnp.where(eye, gram[y * LANES : (y + 1) * LANES, y * LANES : (y + 1) * LANES], 0.0),
            axis=0,
            keepdims=True,
        )
        * row_scale
        for y in range(4)
    ]
    small = jnp.concatenate(rhs + diagonal, axis=0).astype(BF16)
    for y in range(4):
        for x in range(4):
            for core in range(2):
                peer = y * 8 + x * 2 + core
                for zh in range(4):
                    low = x * 128 + zh * 32 + core * 16
                    out_ref[peer, zh * 16 : zh * 16 + 16, :] = (
                        gram[low : low + 16, y * LANES : (y + 1) * LANES] * gram_scale
                    ).astype(BF16)
                out_ref[peer, 64:72, :] = small


def middle_kernel(in_ref, out_ref):
    total = in_ref[0].astype(F32)
    for peer in range(1, in_ref.shape[0]):
        total = total + in_ref[peer].astype(F32)
    small = total[64:72, :].astype(BF16)
    head = total[0:64, :].astype(BF16)
    tail = (total[0:64, :] - head.astype(F32)).astype(BF16)
    for zl in range(4):
        for zh in range(4):
            peer = zl * 4 + zh
            for b in range(4):
                rows = slice(zh * 16 + 4 * b, zh * 16 + 4 * b + 4)
                lanes = slice(zl * 32, zl * 32 + 32)
                out_ref[peer, 0:4, b * 32 : b * 32 + 32] = head[rows, lanes]
                out_ref[peer, 4:8, b * 32 : b * 32 + 32] = tail[rows, lanes]
            out_ref[peer, 8:16, :] = small


def last_kernel(in_ref, normal_ref, rhs_ref, diagonal_ref):
    total = in_ref[0].astype(F32)
    for peer in range(1, in_ref.shape[0]):
        total = total + in_ref[peer].astype(F32)
    tile = total[0:4, :] + total[4:8, :]
    for b in range(4):
        normal_ref[4 * b : 4 * b + 4, :] = tile[:, b * 32 : b * 32 + 32]
    rows, cols = normal_ref.shape
    row_low = (lax.axis_index("zh") * 8 + lax.axis_index("x") * 2 + lax.axis_index("core")) * rows
    col_low = (lax.axis_index("zl") * 4 + lax.axis_index("y")) * cols
    on_diagonal = row_low + iota((rows, cols), 0) == col_low + iota((rows, cols), 1)
    normal_ref[...] = jnp.where(on_diagonal, 0.0, normal_ref[...])
    for out_ref, low in ((rhs_ref, 8), (diagonal_ref, 12)):
        for zl in range(4):
            for y in range(4):
                out_ref[0:1, zl * 128 + y * 32 : zl * 128 + y * 32 + 32] = total[
                    low + y : low + y + 1, zl * 32 : zl * 32 + 32
                ]


def load_kernel(*refs):
    count = (len(refs) - 2) // 2
    sources, packed_ref, targets, sems = refs[:count], refs[count], refs[count + 1 : -1], refs[-1]
    copies = [
        pltpu.make_async_copy(source, target, sems.at[index])
        for index, (source, target) in enumerate(zip(sources, targets))
    ]
    for copy in copies:
        copy.start()
    for copy in copies:
        copy.wait()
    colat_ref, lon_ref, obs_ref, start_ref = targets[:4]
    last = colat_ref.shape[0] - 2
    span = obs_ref.shape[1]
    packed_ref[0:2, :] = colat_ref[last : last + 2, :]
    packed_ref[2:4, :] = lon_ref[last : last + 2, :]
    for component in range(2):
        for half in range(2):
            low = span - (2 - half) * LANES
            row = 4 + 2 * component + half
            packed_ref[row : row + 1, :] = obs_ref[component : component + 1, low : low + LANES].astype(
                F32
            )
    packed_ref[8:10, :] = start_ref[last : last + 2, :].astype(F32)
    packed_ref[10:16, :] = jnp.ones((6, LANES), F32)


def on_device(colatitude, longitude, observed, filter_taps, segment_start, harmonic):
    rows_here = colatitude.shape[0]
    panel = harmonic.shape[1]
    blocks = rows_here // TAPS
    rows_total = rows_here * 512
    vmem = pl.BlockSpec(memory_space=pltpu.VMEM)

    def kernel(body, name, outs, scratch, mebibytes, operands, estimate=None):
        return pl.pallas_call(
            body,
            name=name,
            out_shape=outs,
            in_specs=[vmem] * len(operands),
            out_specs=jax.tree.map(lambda _: vmem, outs),
            scratch_shapes=scratch,
            cost_estimate=estimate,
            compiler_params=pltpu.CompilerParams(vmem_limit_bytes=mebibytes * 1024 * 1024),
        )(*operands)

    colat = colatitude.reshape(-1, LANES)
    lon = longitude.reshape(-1, LANES)
    start = segment_start.reshape(-1, LANES)
    arguments = (colat, lon, observed, start, harmonic, filter_taps)
    packed, colat, lon, observed, start, harmonic, filter_taps = pl.pallas_call(
        load_kernel,
        name="load_and_pack",
        out_shape=(
            jax.ShapeDtypeStruct((16, LANES), F32),
            *(jax.ShapeDtypeStruct(value.shape, value.dtype) for value in arguments),
        ),
        in_specs=[pl.BlockSpec(memory_space=pltpu.HBM)] * len(arguments),
        out_specs=(vmem,) * (len(arguments) + 1),
        scratch_shapes=[pltpu.SemaphoreType.DMA((len(arguments),))],
        compiler_params=pltpu.CompilerParams(vmem_limit_bytes=4 * 1024 * 1024),
    )(*(pltpu.with_memory_space_constraint(value, pltpu.HBM) for value in arguments))
    halo = lax.ppermute(packed, ("zh", "x", "core"), [(i, i + 1) for i in range(31)])
    before, head, columns, toeplitz = kernel(
        own_kernel,
        "own_epochs",
        (
            jax.ShapeDtypeStruct((panel + 16, panel), F32),
            jax.ShapeDtypeStruct((2, panel + 16, TAPS), BF16),
            jax.ShapeDtypeStruct((3, panel, LANES), F32),
            jax.ShapeDtypeStruct((2, 3, LANES, LANES), F32),
        ),
        [
            pltpu.VMEM((2, panel + 16, rows_here), BF16),
            pltpu.VMEM((panel + 16, 2 * (rows_here - TAPS)), BF16),
            pltpu.VMEM((blocks - 1, 2, 2 * TAPS, TAPS), BF16),
            pltpu.VMEM((4, 16, LANES), F32),
            pltpu.VMEM((LANES, LANES), F32),
        ],
        32,
        (colat, lon, observed, start, harmonic, filter_taps),
        pl.CostEstimate(flops=4_000_000_000, bytes_accessed=4_000_000, transcendentals=3_000_000),
    )
    payload = kernel(
        functools.partial(
            edge_kernel, row_scale=1.0 / rows_total, gram_scale=1.0 / math.sqrt(rows_total)
        ),
        "edge_epochs",
        jax.ShapeDtypeStruct((32, 72, LANES), BF16),
        [
            pltpu.VMEM((2, panel + 16, TAPS), BF16),
            pltpu.VMEM((panel + 16, 2 * TAPS), BF16),
            pltpu.VMEM((1, 2, 2 * TAPS, TAPS), BF16),
            pltpu.VMEM((4, 8, LANES), F32),
            pltpu.VMEM((LANES, LANES), F32),
            pltpu.VMEM((panel + 16, panel), F32),
        ],
        16,
        (halo, start, before, head, columns, toeplitz),
    )
    arrived = lax.all_to_all(payload, ("y", "x", "core"), 0, 0)
    sums = kernel(
        middle_kernel, "sum_over_plane", jax.ShapeDtypeStruct((16, 16, LANES), BF16), [], 8, (arrived,)
    )
    gathered = lax.all_to_all(sums, ("zl", "zh"), 0, 0)
    normal, right_side, diagonal = kernel(
        last_kernel,
        "sum_over_z",
        (
            jax.ShapeDtypeStruct((16, 32), F32),
            jax.ShapeDtypeStruct((1, panel), F32),
            jax.ShapeDtypeStruct((1, panel), F32),
        ),
        [],
        8,
        (gathered,),
    )
    return normal, right_side.reshape(panel), diagonal.reshape(panel)


def solution(mesh):
    fine = Mesh(mesh.devices.reshape(4, 4, 4, 4, 2), ("zl", "y", "zh", "x", "core"))
    everywhere = ("zl", "y", "zh", "x", "core")
    return jax.shard_map(
        on_device,
        mesh=fine,
        in_specs=(P(everywhere), P(everywhere), P(None, everywhere), P(), P(everywhere), P()),
        out_specs=(P(("zh", "x", "core"), ("zl", "y")), P(), P()),
        check_vma=False,
    )
```

time: 81.9 us -> 68.7 us (0.84)
  the two profiles are of different devices: /device:TPU:32 before, /device:TPU:1 now
where the time goes in v2:
time: 68.7 us; the launch traced here: 68.4 us
  blocking collectives  46.2 us (67%)
  Pallas kernels  17.1 us (25%)
  starting transfers between devices  4.5 us (7%)
    all_to_all x1, blocking collectives, on_device(): arrived = lax.all_to_all(payload, ('y', 'x', 'core'), 0, 0)  24.5 us
    all_to_all x1, blocking collectives, on_device(): gathered = lax.all_to_all(sums, ('zl', 'zh'), 0, 0)  21.7 us
    pallas_call x4, Pallas kernels, kernel(): pl.pallas_call(body, name=name, out_shape=outs, in_specs=[vmem] * len(ope...  16.3 us
    ppermute x1, starting transfers between devices, on_device(): lax.ppermute(packed, ('zh', 'x', 'core'), [(i, i + 1) for i in range(31)])  4.5 us
  transfers between devices with their start and end apart: 1, of which 0 were waited for; matrix products, arithmetic and copies ran while one was open for 0% of the time, Pallas kernels for 18%

profile of v2, /device:TPU:1, one launch (start us, length us, event | category | flops | bytes accessed | tf_op | source)
XLA Modules:
  0.0 68.4 jit_solution(17909961637919592339)
XLA Ops:
  0.6 0.8 %load_and_pack.1 = (f32[16,128]{1,0:T(8,128)S(1)}, f32[16,128]{1,0:T(8,128)S(1)}, f32[16,128]{1,0:T(8,128)S(1)}, bf16[2,2048]{1,0:T(2,128)(2,1)S(1)}, s32[16,128...) custom-call(f32[16,128]{1,0:T(8,128)} %bitcast.5, f32[16,128]{1,0:T(8,128)} %bitcast.6, ...), custom_call_target="tpu_custom_call" | custom-call | tf_op jit(solution)/shard_map/load_and_pack/pallas_call | solution.py:344
  1.5 4.5 %collective-permute-start = (f32[16,128]{1,0:T(8,128)S(1)}, f32[16,128]{1,0:T(8,128)S(1)}, u32[]{:S(2)}, u32[]{:S(2)}) collective-permute-start(f32[16,128]{1,0:T(8,128)S(1)} %get-tuple-element.17), channel_id=1, source_target_pairs={{0,1},{1,2},{2,3},{3,4},{4,5},{5,6},{6,7},{7,8},{8,9},{9,10},{10,1... | collective-permute-start | bytes 24584 | tf_op jit(solution)/shard_map/ppermute | solution.py:356
  6.0 12.6 %own_epochs.1 = (f32[528,512]{1,0:T(8,128)S(1)}, bf16[2,528,256]{2,1,0:T(8,128)(2,1)S(1)}, f32[3,512,128]{2,1,0:T(8,128)S(1)}, f32[2,3,128,128]{3,2,1,0:T(8,128)S(1)}) custom-call(f32[16,128]{1,0:T(8,128)S(1)} %get-tuple-element.19.colat_ref, f32[16,128]{1,0:T(8,128)S(1)} %get-tuple-element.20.lon_ref, bf16[2,2048]{1,0:T(2,128)(2,1)S(1)} %get-tuple-element.21.obs_ref, ...), custom_call_target="tpu_custom_call" | custom-call | flops 4000000000 | bytes 4000000 | tf_op jit(solution)/shard_map/own_epochs/pallas_call | solution.py:329
  18.5 0.0 collective-permute-done.halo_ref
  18.6 2.7 %edge_epochs.1 = bf16[32,72,128]{2,1,0:T(8,128)(2,1)S(1)} custom-call(f32[16,128]{1,0:T(8,128)S(1)} %collective-permute-done.halo_ref, s32[16,128]{1,0:T(8,128)S(1)} %get-tuple-element.18.start_ref, f32[528,512]{1,0:T(8,128)S(1)} %get-tuple-element.24.before_ref, bf16[2,528,256]{2,1,0:T(8,128)(2,1)S(1)} %get-tuple-element.25.head_ref, ...), custom_call_target="tpu_custom_call" | custom-call | tf_op jit(solution)/shard_map/edge_epochs/pallas_call | solution.py:329
  21.3 24.5 %all_to_all.10.in_ref = bf16[32,72,128]{2,1,0:T(8,128)(2,1)S(1)} all-to-all(bf16[32,72,128]{2,1,0:T(8,128)(2,1)S(1)} %edge_epochs.1), channel_id=1, replica_groups=mesh['zl'=4,'y'=4,'zh'=4,'x'=4,'core'=2] {'y','x','core'}, dimensions={0} | all-to-all | bytes 1179648 | tf_op jit(solution)/shard_map/all_to_all | solution.py:394
  45.8 0.3 sum_over_plane.1
  46.0 21.7 %all_to_all.11.in_ref = bf16[16,16,128]{2,1,0:T(8,128)(2,1)S(1)} all-to-all(bf16[16,16,128]{2,1,0:T(8,128)(2,1)S(1)} %sum_over_plane.1), channel_id=1, replica_groups=mesh['zl'=4,'y'=4,'zh'=4,'x'=4,'core'=2] {'zl','zh'}, dimensions={0} | all-to-all | bytes 131072 | tf_op jit(solution)/shard_map/all_to_all | solution.py:398
  67.7 0.7 %sum_over_z.1 = (f32[16,32]{1,0:T(8,128)}, f32[1,512]{1,0:T(1,128)}, f32[1,512]{1,0:T(1,128)}) custom-call(bf16[16,16,128]{2,1,0:T(8,128)(2,1)S(1)} %all_to_all.11.in_ref), custom_call_target="tpu_custom_call" | custom-call | tf_op jit(solution)/shard_map/sum_over_z/pallas_call | solution.py:329
Async XLA Ops:
  1.5 17.1 %collective-permute-start = (f32[16,128]{1,0:T(8,128)S(1)}, f32[16,128]{1,0:T(8,128)S(1)}, u32[]{:S(2)}, u32[]{:S(2)}) collective-permute-start(f32[16,128]{1,0:T(8,128)S(1)} %get-tuple-element.17), channel_id=1, source_target_pairs={{0,1},{1,2},{2,3},{3,4},{4,5},{5,6},{6,7},{7,8},{8,9},{9,10},{10,1... | collective-permute-start | bytes 24584 | tf_op jit(solution)/shard_map/ppermute | solution.py:356

commit v3 on v2

--- a/solution.py
+++ b/solution.py
@@ -12,6 +12,7 @@
 BF16 = jnp.bfloat16
 LANES = 128
 TAPS = 256
+MULTIPLES = 288
 SIN_COEFFS = (3.141592639, -5.167709953, 2.550074404, -0.5982681334, 0.07760505745)
 COS_COEFFS = (0.9999999504, -4.934792377, 4.058400535, -1.331796279, 0.2195071918)
 TWO_PI_PARTS = (6.28125, 0.0019340515136718750, 1.2556659146854654e-06)
@@ -83,6 +84,55 @@
     lax.fori_loop(0, columns.shape[1] // 16, some_columns, 0)
 
 
+def sine_and_cosine(turns, slot, factor):
+    part = turns[2 * slot] * factor
+    part = (part - nearest(part)) + turns[2 * slot + 1] * factor
+    z = part * part
+    half_sin = part * horner(SIN_COEFFS, z)
+    twice = half_sin + half_sin
+    return twice * horner(COS_COEFFS, z), 1.0 - twice * half_sin
+
+
+def fill_tables(tables, turns, small):
+    rows = turns.shape[1]
+    for slot in range(2):
+        for b in range(16):
+            sine, cosine = sine_and_cosine(turns, slot, float(b))
+            small[slot, 0, b] = cosine
+            small[slot, 1, b] = sine
+
+    def some_multiples(a, carry):
+        for slot, table in enumerate(tables):
+            sine, cosine = sine_and_cosine(turns, slot, (16 * a).astype(F32))
+            for b in range(16):
+                place = pl.ds(pl.multiple_of(a * (16 * rows), 16 * rows) + b * rows, rows)
+                table[0, place, :] = cosine * small[slot, 0, b] - sine * small[slot, 1, b]
+                table[1, place, :] = sine * small[slot, 0, b] + cosine * small[slot, 1, b]
+        return carry
+
+    lax.fori_loop(0, MULTIPLES // 16, some_multiples, 0)
+
+
+def fill_products(products, rows_of, tables):
+    polar, azimuth = tables
+    rows = 8 * products.shape[1]
+
+    def some_columns(group, carry):
+        start = pl.multiple_of(group * 256, 256)
+        for offset in range(32):
+            degree = pl.multiple_of(rows_of[group, offset], rows)
+            order = pl.multiple_of(rows_of[16 + group, offset], rows)
+            wave = azimuth[pl.ds(order, rows), :]
+            place = pl.ds(start + offset * 8, 8)
+            for component in range(2):
+                value = polar[component, pl.ds(degree, rows), :] * wave
+                for half in range(rows // 8):
+                    products[component, half, place, :] = value[8 * half : 8 * half + 8, :]
+        return carry
+
+    lax.fori_loop(0, 16, some_columns, 0)
+
+
 def fill_signal(design, component, panel, values):
     span = values.shape[1]
     design[component, panel : panel + 16, 0:span] = jnp.where(
@@ -125,6 +175,7 @@
     obs_ref,
     start_ref,
     harmonic_ref,
+    scalar_ref,
     taps_ref,
     gram_ref,
     head_ref,
@@ -135,7 +186,15 @@
     matrices,
     turns,
     starts,
+    polar,
+    azimuth,
+    small,
+    products,
+    scalars,
+    scalars_sem,
 ):
+    scalars_copy = pltpu.make_async_copy(scalar_ref, scalars, scalars_sem)
+    scalars_copy.start()
     rows, _ = colat_ref.shape
     panel = harmonic_ref.shape[1]
     blocks = rows // 2
@@ -167,18 +226,28 @@
         rolled = pltpu.roll(spread, 0, 1, stride=1, stride_axis=0)
         for d in range(3):
             toeplitz_ref[component, d] = rolled[:, d * LANES : (d + 1) * LANES]
+    fill_tables((polar, azimuth.reshape(2, MULTIPLES * rows, LANES)), turns, small)
+    scalars_copy.wait()
+    fill_products(products, scalars, (polar, azimuth))
+    for component in range(2):
+        fill_signal(design, component, panel, obs_ref[component : component + 1, :].astype(F32))
+
+    def to_lanes(block):
+        for component in range(2):
+            for row in (2 * block, 2 * block + 1):
+                for low in range(0, panel, 16):
+                    tile = products[component, row // 8, pl.ds(low * 8 + row % 8, 16, stride=8), :]
+                    design[component, low : low + 16, row * LANES : (row + 1) * LANES] = tile.astype(BF16)
+
+    to_lanes(0)
+    for component in range(2):
+        head_ref[component] = design[component, :, 0:TAPS]
     for block in range(blocks - 1):
+        to_lanes(block + 1)
         fill_matrices(
             matrices, block, 2 * block, by_lane, by_sublane, lambda c, d: toeplitz_ref[c, d]
         )
-
-    fill_design(design, columns_ref, turns, rows)
-    for component in range(2):
-        fill_signal(design, component, panel, obs_ref[component : component + 1, :].astype(F32))
-        head_ref[component] = design[component, :, 0:TAPS]
-
-    for component in range(2):
-        for block in range(blocks - 1):
+        for component in range(2):
             window = design[component, :, block * TAPS : block * TAPS + 2 * TAPS]
             low = (component * (blocks - 1) + block) * TAPS
             filtered[:, low : low + TAPS] = dot_nn(window, matrices[block, component]).astype(BF16)
@@ -292,8 +361,9 @@
 
 
 def load_kernel(*refs):
-    count = (len(refs) - 2) // 2
-    sources, packed_ref, targets, sems = refs[:count], refs[count], refs[count + 1 : -1], refs[-1]
+    count = (len(refs) - 3) // 2
+    sources, packed_ref, rows_ref = refs[:count], refs[count], refs[count + 1]
+    targets, sems = refs[count + 2 : -1], refs[-1]
     copies = [
         pltpu.make_async_copy(source, target, sems.at[index])
         for index, (source, target) in enumerate(zip(sources, targets))
@@ -316,6 +386,16 @@
             )
     packed_ref[8:10, :] = start_ref[last : last + 2, :].astype(F32)
     packed_ref[10:16, :] = jnp.ones((6, LANES), F32)
+    rows = colat_ref.shape[0]
+    degree = targets[4][0:1, :]
+    order = targets[4][1:2, :]
+    wave = jnp.abs(order) + jnp.where(order < 0, MULTIPLES, 0)
+    for y in range(4):
+        for zl in range(4):
+            group = y * 4 + zl
+            lanes = slice(zl * LANES + y * 32, zl * LANES + y * 32 + 32)
+            rows_ref[group : group + 1, 0:32] = degree[:, lanes] * rows
+            rows_ref[16 + group : 17 + group, 0:32] = wave[:, lanes] * rows
 
 
 def on_device(colatitude, longitude, observed, filter_taps, segment_start, harmonic):
@@ -324,6 +404,7 @@
     blocks = rows_here // TAPS
     rows_total = rows_here * 512
     vmem = pl.BlockSpec(memory_space=pltpu.VMEM)
+    hbm = pl.BlockSpec(memory_space=pltpu.HBM)
 
     def kernel(body, name, outs, scratch, mebibytes, operands, estimate=None):
         return pl.pallas_call(
@@ -341,15 +422,16 @@
     lon = longitude.reshape(-1, LANES)
     start = segment_start.reshape(-1, LANES)
     arguments = (colat, lon, observed, start, harmonic, filter_taps)
-    packed, colat, lon, observed, start, harmonic, filter_taps = pl.pallas_call(
+    packed, table_rows, colat, lon, observed, start, harmonic, filter_taps = pl.pallas_call(
         load_kernel,
         name="load_and_pack",
         out_shape=(
             jax.ShapeDtypeStruct((16, LANES), F32),
+            jax.ShapeDtypeStruct((32, LANES), jnp.int32),
             *(jax.ShapeDtypeStruct(value.shape, value.dtype) for value in arguments),
         ),
-        in_specs=[pl.BlockSpec(memory_space=pltpu.HBM)] * len(arguments),
-        out_specs=(vmem,) * (len(arguments) + 1),
+        in_specs=[hbm] * len(arguments),
+        out_specs=(vmem,) * (len(arguments) + 2),
         scratch_shapes=[pltpu.SemaphoreType.DMA((len(arguments),))],
         compiler_params=pltpu.CompilerParams(vmem_limit_bytes=4 * 1024 * 1024),
     )(*(pltpu.with_memory_space_constraint(value, pltpu.HBM) for value in arguments))
@@ -367,11 +449,17 @@
             pltpu.VMEM((2, panel + 16, rows_here), BF16),
             pltpu.VMEM((panel + 16, 2 * (rows_here - TAPS)), BF16),
             pltpu.VMEM((blocks - 1, 2, 2 * TAPS, TAPS), BF16),
-            pltpu.VMEM((4, 16, LANES), F32),
+            pltpu.VMEM((4, rows_here // LANES, LANES), F32),
             pltpu.VMEM((LANES, LANES), F32),
+            pltpu.VMEM((2, MULTIPLES * rows_here // LANES, LANES), F32),
+            pltpu.VMEM((2 * MULTIPLES * rows_here // LANES, LANES), F32),
+            pltpu.VMEM((2, 2, 16, rows_here // LANES, LANES), F32),
+            pltpu.VMEM((2, rows_here // LANES // 8, panel * 8, LANES), F32),
+            pltpu.SMEM((32, LANES), jnp.int32),
+            pltpu.SemaphoreType.DMA(()),
         ],
-        32,
-        (colat, lon, observed, start, harmonic, filter_taps),
+        48,
+        (colat, lon, observed, start, harmonic, table_rows, filter_taps),
         pl.CostEstimate(flops=4_000_000_000, bytes_accessed=4_000_000, transcendentals=3_000_000),
     )
     payload = kernel(

time: 68.7 us -> 64.7 us (0.942)
  Pallas kernels: 17.1 us -> 13.1 us
    pallas_call x4, Pallas kernels: 16.3 us -> 12.2 us  [kernel(): pl.pallas_call(body, name=name, out_shape=outs, in_specs=[vmem] * len(ope...]
  transfers between devices with their start and end apart: 1 -> 1, of which waited for: 0 -> 0; matrix products, arithmetic and copies ran while one was open for 0% -> 0% of each run, Pallas kernels for 18% -> 13%
where the time goes in v3:
time: 64.7 us; the launch traced here: 64.5 us
  blocking collectives  46.2 us (71%)
  Pallas kernels  13.1 us (20%)
  starting transfers between devices  4.5 us (7%)
  between operations  0.68 us (1%)
    all_to_all x1, blocking collectives, on_device(): arrived = lax.all_to_all(payload, ('y', 'x', 'core'), 0, 0)  24.5 us
    all_to_all x1, blocking collectives, on_device(): gathered = lax.all_to_all(sums, ('zl', 'zh'), 0, 0)  21.7 us
    pallas_call x4, Pallas kernels, kernel(): pl.pallas_call(body, name=name, out_shape=outs, in_specs=[vmem] * len(ope...  12.2 us
    ppermute x1, starting transfers between devices, on_device(): lax.ppermute(packed, ('zh', 'x', 'core'), [(i, i + 1) for i in range(31)])  4.5 us
  transfers between devices with their start and end apart: 1, of which 0 were waited for; matrix products, arithmetic and copies ran while one was open for 0% of the time, Pallas kernels for 13%

profile of v3, /device:TPU:1, one launch (start us, length us, event | category | flops | bytes accessed | tf_op | source)
XLA Modules:
  0.0 64.5 jit_solution(15642053792252709762)
XLA Ops:
  0.6 0.9 %load_and_pack.1 = (f32[16,128]{1,0:T(8,128)S(1)}, s32[32,128]{1,0:T(8,128)S(1)}, f32[16,128]{1,0:T(8,128)S(1)}, f32[16,128]{1,0:T(8,128)S(1)}, bf16[2,2048]{1,0...) custom-call(f32[16,128]{1,0:T(8,128)} %bitcast.5, f32[16,128]{1,0:T(8,128)} %bitcast.6, ...), custom_call_target="tpu_custom_call" | custom-call | tf_op jit(solution)/shard_map/load_and_pack/pallas_call | solution.py:425
  1.5 4.5 %collective-permute-start = (f32[16,128]{1,0:T(8,128)S(1)}, f32[16,128]{1,0:T(8,128)S(1)}, u32[]{:S(2)}, u32[]{:S(2)}) collective-permute-start(f32[16,128]{1,0:T(8,128)S(1)} %get-tuple-element.18), channel_id=1, source_target_pairs={{0,1},{1,2},{2,3},{3,4},{4,5},{5,6},{6,7},{7,8},{8,9},{9,10},{10,1... | collective-permute-start | bytes 24584 | tf_op jit(solution)/shard_map/ppermute | solution.py:438
  6.0 8.5 %own_epochs.1 = (f32[528,512]{1,0:T(8,128)S(1)}, bf16[2,528,256]{2,1,0:T(8,128)(2,1)S(1)}, f32[3,512,128]{2,1,0:T(8,128)S(1)}, f32[2,3,128,128]{3,2,1,0:T(8,128)S(1)}) custom-call(f32[16,128]{1,0:T(8,128)S(1)} %get-tuple-element.20.colat_ref, f32[16,128]{1,0:T(8,128)S(1)} %get-tuple-element.21.lon_ref, bf16[2,2048]{1,0:T(2,128)(2,1)S(1)} %get-tuple-element.22.obs_ref, ...), custom_call_target="tpu_custom_call" | custom-call | flops 4000000000 | bytes 4000000 | tf_op jit(solution)/shard_map/own_epochs/pallas_call | solution.py:410
  14.6 0.0 collective-permute-done.halo_ref
  14.6 2.7 %edge_epochs.1 = bf16[32,72,128]{2,1,0:T(8,128)(2,1)S(1)} custom-call(f32[16,128]{1,0:T(8,128)S(1)} %collective-permute-done.halo_ref, s32[16,128]{1,0:T(8,128)S(1)} %get-tuple-element.19.start_ref, f32[528,512]{1,0:T(8,128)S(1)} %get-tuple-element.26.before_ref, bf16[2,528,256]{2,1,0:T(8,128)(2,1)S(1)} %get-tuple-element.27.head_ref, ...), custom_call_target="tpu_custom_call" | custom-call | tf_op jit(solution)/shard_map/edge_epochs/pallas_call | solution.py:410
  17.3 24.5 %all_to_all.10.in_ref = bf16[32,72,128]{2,1,0:T(8,128)(2,1)S(1)} all-to-all(bf16[32,72,128]{2,1,0:T(8,128)(2,1)S(1)} %edge_epochs.1), channel_id=1, replica_groups=mesh['zl'=4,'y'=4,'zh'=4,'x'=4,'core'=2] {'y','x','core'}, dimensions={0} | all-to-all | bytes 1179648 | tf_op jit(solution)/shard_map/all_to_all | solution.py:482
  41.8 0.3 sum_over_plane.1
  42.1 21.7 %all_to_all.11.in_ref = bf16[16,16,128]{2,1,0:T(8,128)(2,1)S(1)} all-to-all(bf16[16,16,128]{2,1,0:T(8,128)(2,1)S(1)} %sum_over_plane.1), channel_id=1, replica_groups=mesh['zl'=4,'y'=4,'zh'=4,'x'=4,'core'=2] {'zl','zh'}, dimensions={0} | all-to-all | bytes 131072 | tf_op jit(solution)/shard_map/all_to_all | solution.py:486
  63.8 0.7 %sum_over_z.1 = (f32[16,32]{1,0:T(8,128)}, f32[1,512]{1,0:T(1,128)}, f32[1,512]{1,0:T(1,128)}) custom-call(bf16[16,16,128]{2,1,0:T(8,128)(2,1)S(1)} %all_to_all.11.in_ref), custom_call_target="tpu_custom_call" | custom-call | tf_op jit(solution)/shard_map/sum_over_z/pallas_call | solution.py:410
Async XLA Ops:
  1.5 13.1 %collective-permute-start = (f32[16,128]{1,0:T(8,128)S(1)}, f32[16,128]{1,0:T(8,128)S(1)}, u32[]{:S(2)}, u32[]{:S(2)}) collective-permute-start(f32[16,128]{1,0:T(8,128)S(1)} %get-tuple-element.18), channel_id=1, source_target_pairs={{0,1},{1,2},{2,3},{3,4},{4,5},{5,6},{6,7},{7,8},{8,9},{9,10},{10,1... | collective-permute-start | bytes 24584 | tf_op jit(solution)/shard_map/ppermute | solution.py:438

commit v4 on v3

--- a/solution.py
+++ b/solution.py
@@ -58,10 +58,10 @@
 
 def fill_design(design, columns, turns, chunks):
     def some_columns(step, carry):
-        low = pl.multiple_of(step * 16, 16)
-        degree = columns[0, pl.ds(low, 16), :]
-        order = columns[1, pl.ds(low, 16), :]
-        phase = columns[2, pl.ds(low, 16), :]
+        low = pl.multiple_of(step * 32, 32)
+        degree = columns[0, pl.ds(low, 32), :]
+        order = columns[1, pl.ds(low, 32), :]
+        phase = columns[2, pl.ds(low, 32), :]
         for chunk in range(chunks):
             row = slice(chunk, chunk + 1)
             lane = slice(chunk * LANES, (chunk + 1) * LANES)
@@ -77,11 +77,11 @@
             azimuth = (azimuth - nearest(azimuth)) + order * turns[3, row, :]
             half = azimuth * horner(SIN_COEFFS, azimuth * azimuth)
             wave = 1.0 - (half + half) * half
-            design[0, pl.ds(low, 16), lane] = (cos_polar * wave).astype(BF16)
-            design[1, pl.ds(low, 16), lane] = (sin_polar * wave).astype(BF16)
+            design[0, pl.ds(low, 32), lane] = (cos_polar * wave).astype(BF16)
+            design[1, pl.ds(low, 32), lane] = (sin_polar * wave).astype(BF16)
         return carry
 
-    lax.fori_loop(0, columns.shape[1] // 16, some_columns, 0)
+    lax.fori_loop(0, columns.shape[1] // 32, some_columns, 0)
 
 
 def sine_and_cosine(turns, slot, factor):
@@ -115,19 +115,27 @@
 
 def fill_products(products, rows_of, tables):
     polar, azimuth = tables
-    rows = 8 * products.shape[1]
+    rows = 4 * products.shape[1]
+    upper = iota((8, LANES), 0) >= 4
 
     def some_columns(group, carry):
-        start = pl.multiple_of(group * 256, 256)
-        for offset in range(32):
-            degree = pl.multiple_of(rows_of[group, offset], rows)
-            order = pl.multiple_of(rows_of[16 + group, offset], rows)
-            wave = azimuth[pl.ds(order, rows), :]
-            place = pl.ds(start + offset * 8, 8)
+        start = pl.multiple_of(group * 128, 128)
+        for pair in range(16):
+            values = []
+            for offset in (2 * pair, 2 * pair + 1):
+                degree = pl.multiple_of(rows_of[group, offset], rows)
+                order = pl.multiple_of(rows_of[16 + group, offset], rows)
+                wave = azimuth[pl.ds(order, rows), :]
+                values.append([polar[c, pl.ds(degree, rows), :] * wave for c in range(2)])
+            place = pl.ds(start + pair * 8, 8)
             for component in range(2):
-                value = polar[component, pl.ds(degree, rows), :] * wave
                 for half in range(rows // 8):
-                    products[component, half, place, :] = value[8 * half : 8 * half + 8, :]
+                    one = values[0][component][8 * half : 8 * half + 8, :]
+                    two = values[1][component][8 * half : 8 * half + 8, :]
+                    products[component, 2 * half, place, :] = jnp.where(upper, pltpu.roll(two, 4, 0), one)
+                    products[component, 2 * half + 1, place, :] = jnp.where(
+                        upper, two, pltpu.roll(one, 4, 0)
+                    )
         return carry
 
     lax.fori_loop(0, 16, some_columns, 0)
@@ -236,7 +244,7 @@
         for component in range(2):
             for row in (2 * block, 2 * block + 1):
                 for low in range(0, panel, 16):
-                    tile = products[component, row // 8, pl.ds(low * 8 + row % 8, 16, stride=8), :]
+                    tile = products[component, row // 4, pl.ds(low * 4 + row % 4, 16, stride=4), :]
                     design[component, low : low + 16, row * LANES : (row + 1) * LANES] = tile.astype(BF16)
 
     to_lanes(0)
@@ -454,7 +462,7 @@
             pltpu.VMEM((2, MULTIPLES * rows_here // LANES, LANES), F32),
             pltpu.VMEM((2 * MULTIPLES * rows_here // LANES, LANES), F32),
             pltpu.VMEM((2, 2, 16, rows_here // LANES, LANES), F32),
-            pltpu.VMEM((2, rows_here // LANES // 8, panel * 8, LANES), F32),
+            pltpu.VMEM((2, rows_here // LANES // 4, panel * 4, LANES), F32),
             pltpu.SMEM((32, LANES), jnp.int32),
             pltpu.SemaphoreType.DMA(()),
         ],

time: 64.7 us -> 64 us (0.989)
  Pallas kernels: 13.1 us -> 12.4 us
    pallas_call x4, Pallas kernels: 12.2 us -> 11.5 us  [kernel(): pl.pallas_call(body, name=name, out_shape=outs, in_specs=[vmem] * len(ope...]
where the time goes in v4:
time: 64 us; the launch traced here: 63.7 us
  blocking collectives  46.2 us (72%)
  Pallas kernels  12.4 us (19%)
  starting transfers between devices  4.5 us (7%)
  between operations  0.68 us (1%)
    all_to_all x1, blocking collectives, on_device(): arrived = lax.all_to_all(payload, ('y', 'x', 'core'), 0, 0)  24.5 us
    all_to_all x1, blocking collectives, on_device(): gathered = lax.all_to_all(sums, ('zl', 'zh'), 0, 0)  21.7 us
    pallas_call x4, Pallas kernels, kernel(): pl.pallas_call(body, name=name, out_shape=outs, in_specs=[vmem] * len(ope...  11.5 us
    ppermute x1, starting transfers between devices, on_device(): lax.ppermute(packed, ('zh', 'x', 'core'), [(i, i + 1) for i in range(31)])  4.5 us
  transfers between devices with their start and end apart: 1, of which 0 were waited for; matrix products, arithmetic and copies ran while one was open for 0% of the time, Pallas kernels for 13%

profile of v4, /device:TPU:1, one launch (start us, length us, event | category | flops | bytes accessed | tf_op | source)
XLA Modules:
  0.0 63.7 jit_solution(8352706948550783941)
XLA Ops:
  0.6 0.9 %load_and_pack.1 = (f32[16,128]{1,0:T(8,128)S(1)}, s32[32,128]{1,0:T(8,128)S(1)}, f32[16,128]{1,0:T(8,128)S(1)}, f32[16,128]{1,0:T(8,128)S(1)}, bf16[2,2048]{1,0...) custom-call(f32[16,128]{1,0:T(8,128)} %bitcast.5, f32[16,128]{1,0:T(8,128)} %bitcast.6, ...), custom_call_target="tpu_custom_call" | custom-call | tf_op jit(solution)/shard_map/load_and_pack/pallas_call | solution.py:433
  1.5 4.5 %collective-permute-start = (f32[16,128]{1,0:T(8,128)S(1)}, f32[16,128]{1,0:T(8,128)S(1)}, u32[]{:S(2)}, u32[]{:S(2)}) collective-permute-start(f32[16,128]{1,0:T(8,128)S(1)} %get-tuple-element.18), channel_id=1, source_target_pairs={{0,1},{1,2},{2,3},{3,4},{4,5},{5,6},{6,7},{7,8},{8,9},{9,10},{10,1... | collective-permute-start | bytes 24584 | tf_op jit(solution)/shard_map/ppermute | solution.py:446
  6.0 8.0 %own_epochs.1 = (f32[528,512]{1,0:T(8,128)S(1)}, bf16[2,528,256]{2,1,0:T(8,128)(2,1)S(1)}, f32[3,512,128]{2,1,0:T(8,128)S(1)}, f32[2,3,128,128]{3,2,1,0:T(8,128)S(1)}) custom-call(f32[16,128]{1,0:T(8,128)S(1)} %get-tuple-element.20.colat_ref, f32[16,128]{1,0:T(8,128)S(1)} %get-tuple-element.21.lon_ref, bf16[2,2048]{1,0:T(2,128)(2,1)S(1)} %get-tuple-element.22.obs_ref, ...), custom_call_target="tpu_custom_call" | custom-call | flops 4000000000 | bytes 4000000 | tf_op jit(solution)/shard_map/own_epochs/pallas_call | solution.py:418
  14.1 0.0 collective-permute-done.halo_ref
  14.1 2.5 %edge_epochs.1 = bf16[32,72,128]{2,1,0:T(8,128)(2,1)S(1)} custom-call(f32[16,128]{1,0:T(8,128)S(1)} %collective-permute-done.halo_ref, s32[16,128]{1,0:T(8,128)S(1)} %get-tuple-element.19.start_ref, f32[528,512]{1,0:T(8,128)S(1)} %get-tuple-element.26.before_ref, bf16[2,528,256]{2,1,0:T(8,128)(2,1)S(1)} %get-tuple-element.27.head_ref, ...), custom_call_target="tpu_custom_call" | custom-call | tf_op jit(solution)/shard_map/edge_epochs/pallas_call | solution.py:418
  16.6 24.5 %all_to_all.10.in_ref = bf16[32,72,128]{2,1,0:T(8,128)(2,1)S(1)} all-to-all(bf16[32,72,128]{2,1,0:T(8,128)(2,1)S(1)} %edge_epochs.1), channel_id=1, replica_groups=mesh['zl'=4,'y'=4,'zh'=4,'x'=4,'core'=2] {'y','x','core'}, dimensions={0} | all-to-all | bytes 1179648 | tf_op jit(solution)/shard_map/all_to_all | solution.py:490
  41.1 0.3 sum_over_plane.1
  41.3 21.7 %all_to_all.11.in_ref = bf16[16,16,128]{2,1,0:T(8,128)(2,1)S(1)} all-to-all(bf16[16,16,128]{2,1,0:T(8,128)(2,1)S(1)} %sum_over_plane.1), channel_id=1, replica_groups=mesh['zl'=4,'y'=4,'zh'=4,'x'=4,'core'=2] {'zl','zh'}, dimensions={0} | all-to-all | bytes 131072 | tf_op jit(solution)/shard_map/all_to_all | solution.py:494
  63.0 0.7 %sum_over_z.1 = (f32[16,32]{1,0:T(8,128)}, f32[1,512]{1,0:T(1,128)}, f32[1,512]{1,0:T(1,128)}) custom-call(bf16[16,16,128]{2,1,0:T(8,128)(2,1)S(1)} %all_to_all.11.in_ref), custom_call_target="tpu_custom_call" | custom-call | tf_op jit(solution)/shard_map/sum_over_z/pallas_call | solution.py:418
Async XLA Ops:
  1.5 12.6 %collective-permute-start = (f32[16,128]{1,0:T(8,128)S(1)}, f32[16,128]{1,0:T(8,128)S(1)}, u32[]{:S(2)}, u32[]{:S(2)}) collective-permute-start(f32[16,128]{1,0:T(8,128)S(1)} %get-tuple-element.18), channel_id=1, source_target_pairs={{0,1},{1,2},{2,3},{3,4},{4,5},{5,6},{6,7},{7,8},{8,9},{9,10},{10,1... | collective-permute-start | bytes 24584 | tf_op jit(solution)/shard_map/ppermute | solution.py:446

commit v5 on v4

--- a/solution.py
+++ b/solution.py
@@ -177,13 +177,32 @@
                     matrices[block, component, place[0], place[1]] = jnp.zeros(square, BF16)
 
 
+def products_kernel(
+    *refs,
+    core,
+):
+    colat_ref, lon_ref, scalar_ref = refs[:3]
+    products, turns, polar, azimuth, small, scalars, scalars_sem = refs[-7:]
+    if len(refs) == 12:
+        refs[4][...] = refs[3][...]
+
+    @pl.when(lax.axis_index("core") == core)
+    def _():
+        scalars_copy = pltpu.make_async_copy(scalar_ref, scalars, scalars_sem)
+        scalars_copy.start()
+        rows, _ = colat_ref.shape
+        spread_turns(turns, colat_ref[...], 0, 0)
+        spread_turns(turns, lon_ref[...], 1, 0)
+        fill_tables((polar, azimuth.reshape(2, MULTIPLES * rows, LANES)), turns, small)
+        scalars_copy.wait()
+        fill_products(products, scalars, (polar, azimuth))
+
+
 def own_kernel(
-    colat_ref,
-    lon_ref,
+    products,
     obs_ref,
     start_ref,
     harmonic_ref,
-    scalar_ref,
     taps_ref,
     gram_ref,
     head_ref,
@@ -192,18 +211,9 @@
     design,
     filtered,
     matrices,
-    turns,
     starts,
-    polar,
-    azimuth,
-    small,
-    products,
-    scalars,
-    scalars_sem,
 ):
-    scalars_copy = pltpu.make_async_copy(scalar_ref, scalars, scalars_sem)
-    scalars_copy.start()
-    rows, _ = colat_ref.shape
+    rows, _ = start_ref.shape
     panel = harmonic_ref.shape[1]
     blocks = rows // 2
 
@@ -219,9 +229,6 @@
             columns_ref[1, low : low + 32, :] = jnp.abs(order)
             columns_ref[2, low : low + 32, :] = jnp.where(order < 0.0, 0.25, 0.0)
 
-    spread_turns(turns, colat_ref[...], 0, 0)
-    spread_turns(turns, lon_ref[...], 1, 0)
-
     starts[...] = jnp.zeros_like(starts)
     starts[0:rows, :] = start_ref[...].astype(F32)
     by_lane, by_sublane = labels_of(starts[...].astype(BF16))
@@ -234,9 +241,6 @@
         rolled = pltpu.roll(spread, 0, 1, stride=1, stride_axis=0)
         for d in range(3):
             toeplitz_ref[component, d] = rolled[:, d * LANES : (d + 1) * LANES]
-    fill_tables((polar, azimuth.reshape(2, MULTIPLES * rows, LANES)), turns, small)
-    scalars_copy.wait()
-    fill_products(products, scalars, (polar, azimuth))
     for component in range(2):
         fill_signal(design, component, panel, obs_ref[component : component + 1, :].astype(F32))
 
@@ -263,7 +267,8 @@
 
 
 def edge_kernel(
-    halo_ref,
+    near_ref,
+    far_ref,
     start_ref,
     before_ref,
     head_ref,
@@ -276,11 +281,13 @@
     turns,
     starts,
     gram,
+    halo_ref,
     *,
     row_scale,
     gram_scale,
 ):
     panel = columns_ref.shape[1]
+    halo_ref[...] = near_ref[...] + far_ref[...]
     spread_turns(turns, halo_ref[0:2, :], 0, 0)
     spread_turns(turns, halo_ref[2:4, :], 1, 0)
 
@@ -443,7 +450,39 @@
         scratch_shapes=[pltpu.SemaphoreType.DMA((len(arguments),))],
         compiler_params=pltpu.CompilerParams(vmem_limit_bytes=4 * 1024 * 1024),
     )(*(pltpu.with_memory_space_constraint(value, pltpu.HBM) for value in arguments))
-    halo = lax.ppermute(packed, ("zh", "x", "core"), [(i, i + 1) for i in range(31)])
+    ring = ("zh", "x", "core")
+    halo_near = lax.ppermute(packed, ring, [(i, i + 1) for i in range(0, 31, 2)])
+    sub_rows = rows_here // LANES
+
+    def products_on(core, *before):
+        operands = (colat, lon, table_rows, *(before or (packed,)))
+        outs = [jax.ShapeDtypeStruct((2, sub_rows // 4, panel * 4, LANES), F32)]
+        if not before:
+            outs.insert(0, jax.ShapeDtypeStruct((16, LANES), F32))
+        return pl.pallas_call(
+            functools.partial(products_kernel, core=core),
+            name=f"products_on_core_{core}",
+            out_shape=outs,
+            in_specs=[vmem] * len(operands),
+            out_specs=[vmem] * len(outs),
+            scratch_shapes=[
+                pltpu.VMEM((4, sub_rows, LANES), F32),
+                pltpu.VMEM((2, MULTIPLES * sub_rows, LANES), F32),
+                pltpu.VMEM((2 * MULTIPLES * sub_rows, LANES), F32),
+                pltpu.VMEM((2, 2, 16, sub_rows, LANES), F32),
+                pltpu.SMEM((32, LANES), jnp.int32),
+                pltpu.SemaphoreType.DMA(()),
+            ],
+            input_output_aliases={3: 0} if before else {},
+            cost_estimate=pl.CostEstimate(
+                flops=40_000_000, bytes_accessed=8_000_000, transcendentals=0
+            ),
+            compiler_params=pltpu.CompilerParams(vmem_limit_bytes=16 * 1024 * 1024),
+        )(*operands)
+
+    packed_again, products = products_on(1)
+    halo_far = lax.ppermute(packed_again, ring, [(i, i + 1) for i in range(1, 31, 2)])
+    (products,) = products_on(0, products)
     before, head, columns, toeplitz = kernel(
         own_kernel,
         "own_epochs",
@@ -457,18 +496,11 @@
             pltpu.VMEM((2, panel + 16, rows_here), BF16),
             pltpu.VMEM((panel + 16, 2 * (rows_here - TAPS)), BF16),
             pltpu.VMEM((blocks - 1, 2, 2 * TAPS, TAPS), BF16),
-            pltpu.VMEM((4, rows_here // LANES, LANES), F32),
             pltpu.VMEM((LANES, LANES), F32),
-            pltpu.VMEM((2, MULTIPLES * rows_here // LANES, LANES), F32),
-            pltpu.VMEM((2 * MULTIPLES * rows_here // LANES, LANES), F32),
-            pltpu.VMEM((2, 2, 16, rows_here // LANES, LANES), F32),
-            pltpu.VMEM((2, rows_here // LANES // 4, panel * 4, LANES), F32),
-            pltpu.SMEM((32, LANES), jnp.int32),
-            pltpu.SemaphoreType.DMA(()),
         ],
-        48,
-        (colat, lon, observed, start, harmonic, table_rows, filter_taps),
-        pl.CostEstimate(flops=4_000_000_000, bytes_accessed=4_000_000, transcendentals=3_000_000),
+        24,
+        (products, observed, start, harmonic, filter_taps),
+        pl.CostEstimate(flops=4_000_000_000, bytes_accessed=4_000_000, transcendentals=0),
     )
     payload = kernel(
         functools.partial(
@@ -483,9 +515,10 @@
             pltpu.VMEM((4, 8, LANES), F32),
             pltpu.VMEM((LANES, LANES), F32),
             pltpu.VMEM((panel + 16, panel), F32),
+            pltpu.VMEM((16, LANES), F32),
         ],
         16,
-        (halo, start, before, head, columns, toeplitz),
+        (halo_near, halo_far, start, before, head, columns, toeplitz),
     )
     arrived = lax.all_to_all(payload, ("y", "x", "core"), 0, 0)
     sums = kernel(

time: 64 us -> 63.5 us (level)
  starting transfers between devices: 4.5 us -> 3.38 us
    pallas_call x0 -> x2, Pallas kernels: none -> 2.9 us  [products_on(): pl.pallas_call(functools.partial(products_kernel, core=core), name=f'prod...]
    pallas_call x4, Pallas kernels: 11.5 us -> 8.65 us  [kernel(): pl.pallas_call(body, name=name, out_shape=outs, in_specs=[vmem] * len(ope...]
    ppermute x1 -> x2, starting transfers between devices: 4.5 us -> 3.38 us  [the longest x1 2.09 us: on_device(): lax.ppermute(packed_again, ring, [(i, i + 1) for i in range(1, 31, 2)])]
  transfers between devices with their start and end apart: 1 -> 2, of which waited for: 0 -> 0; matrix products, arithmetic and copies ran while one was open for 0% -> 0% of each run, Pallas kernels for 13% -> 13%
where the time goes in v5:
time: 63.5 us; the launch traced here: 63.2 us
  blocking collectives  46.7 us (74%)
  Pallas kernels  12.4 us (20%)
  starting transfers between devices  3.38 us (5%)
  between operations  0.71 us (1%)
    all_to_all x1, blocking collectives, on_device(): arrived = lax.all_to_all(payload, ('y', 'x', 'core'), 0, 0)  24.5 us
    all_to_all x1, blocking collectives, on_device(): gathered = lax.all_to_all(sums, ('zl', 'zh'), 0, 0)  22.2 us
    pallas_call x4, Pallas kernels, kernel(): pl.pallas_call(body, name=name, out_shape=outs, in_specs=[vmem] * len(ope...  8.65 us
    pallas_call x2, Pallas kernels, products_on(): pl.pallas_call(functools.partial(products_kernel, core=core), name=f'prod...  2.9 us
    ppermute x1, starting transfers between devices, on_device(): lax.ppermute(packed_again, ring, [(i, i + 1) for i in range(1, 31, 2)])  2.09 us
    ppermute x1, starting transfers between devices, on_device(): lax.ppermute(packed, ring, [(i, i + 1) for i in range(0, 31, 2)])  1.29 us
  transfers between devices with their start and end apart: 2, of which 0 were waited for; matrix products, arithmetic and copies ran while one was open for 0% of the time, Pallas kernels for 13%

profile of v5, /device:TPU:1, one launch (start us, length us, event | category | flops | bytes accessed | tf_op | source)
XLA Modules:
  0.0 63.2 jit_solution(6197355785582828380)
XLA Ops:
  0.6 0.9 %load_and_pack.1 = (f32[16,128]{1,0:T(8,128)S(1)}, s32[32,128]{1,0:T(8,128)S(1)}, f32[16,128]{1,0:T(8,128)S(1)}, f32[16,128]{1,0:T(8,128)S(1)}, bf16[2,2048]{1,0...) custom-call(f32[16,128]{1,0:T(8,128)} %bitcast.5, f32[16,128]{1,0:T(8,128)} %bitcast.6, ...), custom_call_target="tpu_custom_call" | custom-call | tf_op jit(solution)/shard_map/load_and_pack/pallas_call | solution.py:440
  1.5 1.3 %collective-permute-start = (f32[16,128]{1,0:T(8,128)S(1)}, f32[16,128]{1,0:T(8,128)S(1)}, u32[]{:S(2)}, u32[]{:S(2)}) collective-permute-start(f32[16,128]{1,0:T(8,128)S(1)} %get-tuple-element.20.refs_3_), channel_id=1, source_target_pairs={{0,1},{2,3},{4,5},{6,7},{8,9},{10,11},{12,13},{14,15},{16,17},{18,... | collective-permute-start | bytes 24584 | tf_op jit(solution)/shard_map/ppermute | solution.py:454
  2.8 2.9 %products_on_core_1.1 = (f32[16,128]{1,0:T(8,128)S(1)}, f32[2,4,2048,128]{3,2,1,0:T(8,128)S(1)}) custom-call(f32[16,128]{1,0:T(8,128)S(1)} %get-tuple-element.21.refs_0_, f32[16,128]{1,0:T(8,128)S(1)} %get-tuple-element.22.refs_1_, s32[32,128]{1,0:T(8,128)S(1)} %get-tuple-element.23.refs_2_, f32[16,128]{1,0:T(8,128)S(1)} %get-tuple-element.20.refs_3_), custom_call_target="tpu_custom_call" | custom-call | flops 40000000 | bytes 8000000 | tf_op jit(solution)/shard_map/products_on_core_1/pallas_call | solution.py:462
  5.7 2.1 %collective-permute-start.1 = (f32[16,128]{1,0:T(8,128)S(1)}, f32[16,128]{1,0:T(8,128)S(1)}, u32[]{:S(2)}, u32[]{:S(2)}) collective-permute-start(f32[16,128]{1,0:T(8,128)S(1)} %get-tuple-element.24), channel_id=1, source_target_pairs={{1,2},{3,4},{5,6},{7,8},{9,10},{11,12},{13,14},{15,16},{17,18},{19... | collective-permute-start | bytes 24584 | tf_op jit(solution)/shard_map/ppermute | solution.py:484
  7.8 5.2 %own_epochs.1 = (f32[528,512]{1,0:T(8,128)S(1)}, bf16[2,528,256]{2,1,0:T(8,128)(2,1)S(1)}, f32[3,512,128]{2,1,0:T(8,128)S(1)}, f32[2,3,128,128]{3,2,1,0:T(8,128)S(1)}) custom-call(f32[2,4,2048,128]{3,2,1,0:T(8,128)S(1)} %products_on_core_0.1.products, bf16[2,2048]{1,0:T(2,128)(2,1)S(1)} %get-tuple-element.27.obs_ref, ...), custom_call_target="tpu_custom_call" | custom-call | flops 4000000000 | bytes 4000000 | tf_op jit(solution)/shard_map/own_epochs/pallas_call | solution.py:425
  13.1 0.0 collective-permute-done.near_ref
  13.1 0.0 collective-permute-done.1.far_ref
  13.1 2.5 %edge_epochs.1 = bf16[32,72,128]{2,1,0:T(8,128)(2,1)S(1)} custom-call(f32[16,128]{1,0:T(8,128)S(1)} %collective-permute-done.near_ref, f32[16,128]{1,0:T(8,128)S(1)} %collective-permute-done.1.far_ref, s32[16,128]{1,0:T(8,128)S(1)} %get-tuple-element.25.start_ref, f32[528,512]{1,0:T(8,128)S(1)} %get-tuple-element.30.before_ref, ...), custom_call_target="tpu_custom_call" | custom-call | tf_op jit(solution)/shard_map/edge_epochs/pallas_call | solution.py:425
  15.6 24.5 %all_to_all.10.in_ref = bf16[32,72,128]{2,1,0:T(8,128)(2,1)S(1)} all-to-all(bf16[32,72,128]{2,1,0:T(8,128)(2,1)S(1)} %edge_epochs.1), channel_id=1, replica_groups=mesh['zl'=4,'y'=4,'zh'=4,'x'=4,'core'=2] {'y','x','core'}, dimensions={0} | all-to-all | bytes 1179648 | tf_op jit(solution)/shard_map/all_to_all | solution.py:523
  40.1 0.3 sum_over_plane.1
  40.3 22.2 %all_to_all.11.in_ref = bf16[16,16,128]{2,1,0:T(8,128)(2,1)S(1)} all-to-all(bf16[16,16,128]{2,1,0:T(8,128)(2,1)S(1)} %sum_over_plane.1), channel_id=1, replica_groups=mesh['zl'=4,'y'=4,'zh'=4,'x'=4,'core'=2] {'zl','zh'}, dimensions={0} | all-to-all | bytes 131072 | tf_op jit(solution)/shard_map/all_to_all | solution.py:527
  62.5 0.7 %sum_over_z.1 = (f32[16,32]{1,0:T(8,128)}, f32[1,512]{1,0:T(1,128)}, f32[1,512]{1,0:T(1,128)}) custom-call(bf16[16,16,128]{2,1,0:T(8,128)(2,1)S(1)} %all_to_all.11.in_ref), custom_call_target="tpu_custom_call" | custom-call | tf_op jit(solution)/shard_map/sum_over_z/pallas_call | solution.py:425
  (1 shorter events, 0.0 us)
Async XLA Ops:
  1.5 11.5 %collective-permute-start = (f32[16,128]{1,0:T(8,128)S(1)}, f32[16,128]{1,0:T(8,128)S(1)}, u32[]{:S(2)}, u32[]{:S(2)}) collective-permute-start(f32[16,128]{1,0:T(8,128)S(1)} %get-tuple-element.20.refs_3_), channel_id=1, source_target_pairs={{0,1},{2,3},{4,5},{6,7},{8,9},{10,11},{12,13},{14,15},{16,17},{18,... | collective-permute-start | bytes 24584 | tf_op jit(solution)/shard_map/ppermute | solution.py:454
  5.7 7.4 %collective-permute-start.1 = (f32[16,128]{1,0:T(8,128)S(1)}, f32[16,128]{1,0:T(8,128)S(1)}, u32[]{:S(2)}, u32[]{:S(2)}) collective-permute-start(f32[16,128]{1,0:T(8,128)S(1)} %get-tuple-element.24), channel_id=1, source_target_pairs={{1,2},{3,4},{5,6},{7,8},{9,10},{11,12},{13,14},{15,16},{17,18},{19... | collective-permute-start | bytes 24584 | tf_op jit(solution)/shard_map/ppermute | solution.py:484

commit v6 on v5

--- a/solution.py
+++ b/solution.py
@@ -198,6 +198,13 @@
         fill_products(products, scalars, (polar, azimuth))
 
 
+def three_quadrants(filtered, panel):
+    half = panel // 2
+    upper = jnp.concatenate([filtered[0:half, :], filtered[panel : panel + 16, :]], axis=0)
+    lower = filtered[half:panel, :]
+    return dot_nt(upper, filtered[0:panel, :]), dot_nt(lower, lower)
+
+
 def own_kernel(
     products,
     obs_ref,
@@ -263,7 +270,10 @@
             window = design[component, :, block * TAPS : block * TAPS + 2 * TAPS]
             low = (component * (blocks - 1) + block) * TAPS
             filtered[:, low : low + TAPS] = dot_nn(window, matrices[block, component]).astype(BF16)
-    gram_ref[...] = dot_nt(filtered[...], filtered[0:panel, :])
+    upper, lower = three_quadrants(filtered, panel)
+    half = panel // 2
+    gram_ref[0 : half + 16, :] = upper
+    gram_ref[half + 16 : panel + 16, half:panel] = lower
 
 
 def edge_kernel(
@@ -311,7 +321,13 @@
         )
         filtered[:, component * TAPS : (component + 1) * TAPS] = sums.astype(BF16)
 
-    gram[...] = before_ref[...] + dot_nt(filtered[...], filtered[0:panel, :])
+    upper, lower = three_quadrants(filtered, panel)
+    half = panel // 2
+    upper = upper + before_ref[0 : half + 16, :]
+    gram[0:half, :] = upper[0:half, :]
+    gram[panel : panel + 16, :] = upper[half : half + 16, :]
+    gram[half:panel, half:panel] = lower + before_ref[half + 16 : panel + 16, half:panel]
+    gram[half:panel, 0:half] = jnp.transpose(upper[0:half, half:panel])
 
     eye = iota(square, 0) == iota(square, 1)
     rhs = [gram[panel : panel + 1, y * LANES : (y + 1) * LANES] * gram_scale for y in range(4)]
@@ -341,37 +357,37 @@
     total = in_ref[0].astype(F32)
     for peer in range(1, in_ref.shape[0]):
         total = total + in_ref[peer].astype(F32)
-    small = total[64:72, :].astype(BF16)
-    head = total[0:64, :].astype(BF16)
-    tail = (total[0:64, :] - head.astype(F32)).astype(BF16)
+    rounded = total.astype(BF16)
     for zl in range(4):
         for zh in range(4):
-            peer = zl * 4 + zh
+            low = 3 * (zl * 4 + zh)
             for b in range(4):
-                rows = slice(zh * 16 + 4 * b, zh * 16 + 4 * b + 4)
-                lanes = slice(zl * 32, zl * 32 + 32)
-                out_ref[peer, 0:4, b * 32 : b * 32 + 32] = head[rows, lanes]
-                out_ref[peer, 4:8, b * 32 : b * 32 + 32] = tail[rows, lanes]
-            out_ref[peer, 8:16, :] = small
+                out_ref[low, :, b * 32 : b * 32 + 32] = rounded[
+                    zh * 16 + 4 * b : zh * 16 + 4 * b + 4, zl * 32 : zl * 32 + 32
+                ]
+            out_ref[low + 1] = rounded[64:68, :]
+            out_ref[low + 2] = rounded[68:72, :]
 
 
 def last_kernel(in_ref, normal_ref, rhs_ref, diagonal_ref):
-    total = in_ref[0].astype(F32)
-    for peer in range(1, in_ref.shape[0]):
-        total = total + in_ref[peer].astype(F32)
-    tile = total[0:4, :] + total[4:8, :]
+    totals = []
+    for part in range(3):
+        total = in_ref[part].astype(F32)
+        for peer in range(1, in_ref.shape[0] // 3):
+            total = total + in_ref[3 * peer + part].astype(F32)
+        totals.append(total)
     for b in range(4):
-        normal_ref[4 * b : 4 * b + 4, :] = tile[:, b * 32 : b * 32 + 32]
+        normal_ref[4 * b : 4 * b + 4, :] = totals[0][:, b * 32 : b * 32 + 32]
     rows, cols = normal_ref.shape
     row_low = (lax.axis_index("zh") * 8 + lax.axis_index("x") * 2 + lax.axis_index("core")) * rows
     col_low = (lax.axis_index("zl") * 4 + lax.axis_index("y")) * cols
     on_diagonal = row_low + iota((rows, cols), 0) == col_low + iota((rows, cols), 1)
     normal_ref[...] = jnp.where(on_diagonal, 0.0, normal_ref[...])
-    for out_ref, low in ((rhs_ref, 8), (diagonal_ref, 12)):
+    for out_ref, total in ((rhs_ref, totals[1]), (diagonal_ref, totals[2])):
         for zl in range(4):
             for y in range(4):
                 out_ref[0:1, zl * 128 + y * 32 : zl * 128 + y * 32 + 32] = total[
-                    low + y : low + y + 1, zl * 32 : zl * 32 + 32
+                    y : y + 1, zl * 32 : zl * 32 + 32
                 ]
 
 
@@ -522,9 +538,9 @@
     )
     arrived = lax.all_to_all(payload, ("y", "x", "core"), 0, 0)
     sums = kernel(
-        middle_kernel, "sum_over_plane", jax.ShapeDtypeStruct((16, 16, LANES), BF16), [], 8, (arrived,)
+        middle_kernel, "sum_over_plane", jax.ShapeDtypeStruct((48, 4, LANES), BF16), [], 8, (arrived,)
     )
-    gathered = lax.all_to_all(sums, ("zl", "zh"), 0, 0)
+    gathered = lax.all_to_all(sums, ("zl", "zh"), 0, 0, tiled=True)
     normal, right_side, diagonal = kernel(
         last_kernel,
         "sum_over_z",

time: 63.5 us -> 62.8 us (0.989)
  transfers between devices with their start and end apart: 2 -> 2, of which waited for: 0 -> 0; matrix products, arithmetic and copies ran while one was open for 0% -> 0% of each run, Pallas kernels for 13% -> 12%
where the time goes in v6:
time: 62.8 us; the launch traced here: 62.6 us
  blocking collectives  46.6 us (74%)
  Pallas kernels  11.9 us (19%)
  starting transfers between devices  3.38 us (5%)
  between operations  0.7 us (1%)
    all_to_all x1, blocking collectives, on_device(): arrived = lax.all_to_all(payload, ('y', 'x', 'core'), 0, 0)  24.5 us
    all_to_all x1, blocking collectives, on_device(): gathered = lax.all_to_all(sums, ('zl', 'zh'), 0, 0, tiled=True)  22.1 us
    pallas_call x4, Pallas kernels, kernel(): pl.pallas_call(body, name=name, out_shape=outs, in_specs=[vmem] * len(ope...  8.06 us
    pallas_call x2, Pallas kernels, products_on(): pl.pallas_call(functools.partial(products_kernel, core=core), name=f'prod...  2.9 us
    ppermute x1, starting transfers between devices, on_device(): lax.ppermute(packed_again, ring, [(i, i + 1) for i in range(1, 31, 2)])  2.09 us
    ppermute x1, starting transfers between devices, on_device(): lax.ppermute(packed, ring, [(i, i + 1) for i in range(0, 31, 2)])  1.29 us
  transfers between devices with their start and end apart: 2, of which 0 were waited for; matrix products, arithmetic and copies ran while one was open for 0% of the time, Pallas kernels for 12%

profile of v6, /device:TPU:1, one launch (start us, length us, event | category | flops | bytes accessed | tf_op | source)
XLA Modules:
  0.0 62.6 jit_solution(16142775379154617556)
XLA Ops:
  0.6 0.9 %load_and_pack.1 = (f32[16,128]{1,0:T(8,128)S(1)}, s32[32,128]{1,0:T(8,128)S(1)}, f32[16,128]{1,0:T(8,128)S(1)}, f32[16,128]{1,0:T(8,128)S(1)}, bf16[2,2048]{1,0...) custom-call(f32[16,128]{1,0:T(8,128)} %bitcast.5, f32[16,128]{1,0:T(8,128)} %bitcast.6, ...), custom_call_target="tpu_custom_call" | custom-call | tf_op jit(solution)/shard_map/load_and_pack/pallas_call | solution.py:456
  1.5 1.3 %collective-permute-start = (f32[16,128]{1,0:T(8,128)S(1)}, f32[16,128]{1,0:T(8,128)S(1)}, u32[]{:S(2)}, u32[]{:S(2)}) collective-permute-start(f32[16,128]{1,0:T(8,128)S(1)} %get-tuple-element.20.refs_3_), channel_id=1, source_target_pairs={{0,1},{2,3},{4,5},{6,7},{8,9},{10,11},{12,13},{14,15},{16,17},{18,... | collective-permute-start | bytes 24584 | tf_op jit(solution)/shard_map/ppermute | solution.py:470
  2.8 2.9 %products_on_core_1.1 = (f32[16,128]{1,0:T(8,128)S(1)}, f32[2,4,2048,128]{3,2,1,0:T(8,128)S(1)}) custom-call(f32[16,128]{1,0:T(8,128)S(1)} %get-tuple-element.21.refs_0_, f32[16,128]{1,0:T(8,128)S(1)} %get-tuple-element.22.refs_1_, s32[32,128]{1,0:T(8,128)S(1)} %get-tuple-element.23.refs_2_, f32[16,128]{1,0:T(8,128)S(1)} %get-tuple-element.20.refs_3_), custom_call_target="tpu_custom_call" | custom-call | flops 40000000 | bytes 8000000 | tf_op jit(solution)/shard_map/products_on_core_1/pallas_call | solution.py:478
  5.7 2.1 %collective-permute-start.1 = (f32[16,128]{1,0:T(8,128)S(1)}, f32[16,128]{1,0:T(8,128)S(1)}, u32[]{:S(2)}, u32[]{:S(2)}) collective-permute-start(f32[16,128]{1,0:T(8,128)S(1)} %get-tuple-element.24), channel_id=1, source_target_pairs={{1,2},{3,4},{5,6},{7,8},{9,10},{11,12},{13,14},{15,16},{17,18},{19... | collective-permute-start | bytes 24584 | tf_op jit(solution)/shard_map/ppermute | solution.py:500
  7.8 4.8 %own_epochs.1 = (f32[528,512]{1,0:T(8,128)S(1)}, bf16[2,528,256]{2,1,0:T(8,128)(2,1)S(1)}, f32[3,512,128]{2,1,0:T(8,128)S(1)}, f32[2,3,128,128]{3,2,1,0:T(8,128)S(1)}) custom-call(f32[2,4,2048,128]{3,2,1,0:T(8,128)S(1)} %products_on_core_0.1.products, bf16[2,2048]{1,0:T(2,128)(2,1)S(1)} %get-tuple-element.27.obs_ref, ...), custom_call_target="tpu_custom_call" | custom-call | flops 4000000000 | bytes 4000000 | tf_op jit(solution)/shard_map/own_epochs/pallas_call | solution.py:441
  12.6 0.0 collective-permute-done.near_ref
  12.6 0.0 collective-permute-done.1.far_ref
  12.6 2.4 %edge_epochs.1 = bf16[32,72,128]{2,1,0:T(8,128)(2,1)S(1)} custom-call(f32[16,128]{1,0:T(8,128)S(1)} %collective-permute-done.near_ref, f32[16,128]{1,0:T(8,128)S(1)} %collective-permute-done.1.far_ref, s32[16,128]{1,0:T(8,128)S(1)} %get-tuple-element.25.start_ref, f32[528,512]{1,0:T(8,128)S(1)} %get-tuple-element.30.before_ref, ...), custom_call_target="tpu_custom_call" | custom-call | tf_op jit(solution)/shard_map/edge_epochs/pallas_call | solution.py:441
  15.0 24.5 %all_to_all.10.in_ref = bf16[32,72,128]{2,1,0:T(8,128)(2,1)S(1)} all-to-all(bf16[32,72,128]{2,1,0:T(8,128)(2,1)S(1)} %edge_epochs.1), channel_id=1, replica_groups=mesh['zl'=4,'y'=4,'zh'=4,'x'=4,'core'=2] {'y','x','core'}, dimensions={0} | all-to-all | bytes 1179648 | tf_op jit(solution)/shard_map/all_to_all | solution.py:539
  39.5 0.2 sum_over_plane.1
  39.7 22.1 %all_to_all.11.in_ref = bf16[48,4,128]{2,1,0:T(4,128)(2,1)S(1)} all-to-all(bf16[48,4,128]{2,1,0:T(4,128)(2,1)S(1)} %sum_over_plane.1), channel_id=1, replica_groups=mesh['zl'=4,'y'=4,'zh'=4,'x'=4,'core'=2] {'zl','zh'}, dimensions={0} | all-to-all | bytes 98304 | tf_op jit(solution)/shard_map/all_to_all | solution.py:543
  61.9 0.7 %sum_over_z.1 = (f32[16,32]{1,0:T(8,128)}, f32[1,512]{1,0:T(1,128)}, f32[1,512]{1,0:T(1,128)}) custom-call(bf16[48,4,128]{2,1,0:T(4,128)(2,1)S(1)} %all_to_all.11.in_ref), custom_call_target="tpu_custom_call" | custom-call | tf_op jit(solution)/shard_map/sum_over_z/pallas_call | solution.py:441
  (1 shorter events, 0.0 us)
Async XLA Ops:
  1.5 11.1 %collective-permute-start = (f32[16,128]{1,0:T(8,128)S(1)}, f32[16,128]{1,0:T(8,128)S(1)}, u32[]{:S(2)}, u32[]{:S(2)}) collective-permute-start(f32[16,128]{1,0:T(8,128)S(1)} %get-tuple-element.20.refs_3_), channel_id=1, source_target_pairs={{0,1},{2,3},{4,5},{6,7},{8,9},{10,11},{12,13},{14,15},{16,17},{18,... | collective-permute-start | bytes 24584 | tf_op jit(solution)/shard_map/ppermute | solution.py:470
  5.7 6.9 %collective-permute-start.1 = (f32[16,128]{1,0:T(8,128)S(1)}, f32[16,128]{1,0:T(8,128)S(1)}, u32[]{:S(2)}, u32[]{:S(2)}) collective-permute-start(f32[16,128]{1,0:T(8,128)S(1)} %get-tuple-element.24), channel_id=1, source_target_pairs={{1,2},{3,4},{5,6},{7,8},{9,10},{11,12},{13,14},{15,16},{17,18},{19... | collective-permute-start | bytes 24584 | tf_op jit(solution)/shard_map/ppermute | solution.py:500

commit v7 on v6

--- a/solution.py
+++ b/solution.py
@@ -7,6 +7,7 @@
 from jax.experimental import pallas as pl
 from jax.experimental.pallas import tpu as pltpu
 from jax.sharding import Mesh, PartitionSpec as P
+
 
 F32 = jnp.float32
 BF16 = jnp.bfloat16
@@ -182,9 +183,9 @@
     core,
 ):
     colat_ref, lon_ref, scalar_ref = refs[:3]
-    products, turns, polar, azimuth, small, scalars, scalars_sem = refs[-7:]
-    if len(refs) == 12:
-        refs[4][...] = refs[3][...]
+    packed_ref = refs[3]
+    packed_out, products, turns, polar, azimuth, small, scalars, scalars_sem = refs[-8:]
+    packed_out[...] = packed_ref[...]
 
     @pl.when(lax.axis_index("core") == core)
     def _():
@@ -437,10 +438,9 @@
     vmem = pl.BlockSpec(memory_space=pltpu.VMEM)
     hbm = pl.BlockSpec(memory_space=pltpu.HBM)
 
-    def kernel(body, name, outs, scratch, mebibytes, operands, estimate=None):
+    def kernel(body, outs, scratch, mebibytes, operands, estimate=None):
         return pl.pallas_call(
             body,
-            name=name,
             out_shape=outs,
             in_specs=[vmem] * len(operands),
             out_specs=jax.tree.map(lambda _: vmem, outs),
@@ -467,20 +467,19 @@
         compiler_params=pltpu.CompilerParams(vmem_limit_bytes=4 * 1024 * 1024),
     )(*(pltpu.with_memory_space_constraint(value, pltpu.HBM) for value in arguments))
     ring = ("zh", "x", "core")
-    halo_near = lax.ppermute(packed, ring, [(i, i + 1) for i in range(0, 31, 2)])
     sub_rows = rows_here // LANES
 
     def products_on(core, *before):
-        operands = (colat, lon, table_rows, *(before or (packed,)))
-        outs = [jax.ShapeDtypeStruct((2, sub_rows // 4, panel * 4, LANES), F32)]
-        if not before:
-            outs.insert(0, jax.ShapeDtypeStruct((16, LANES), F32))
+        operands = (colat, lon, table_rows, packed, *before)
+        outs = (
+            jax.ShapeDtypeStruct((16, LANES), F32),
+            jax.ShapeDtypeStruct((2, sub_rows // 4, panel * 4, LANES), F32),
+        )
         return pl.pallas_call(
             functools.partial(products_kernel, core=core),
-            name=f"products_on_core_{core}",
             out_shape=outs,
             in_specs=[vmem] * len(operands),
-            out_specs=[vmem] * len(outs),
+            out_specs=(vmem, vmem),
             scratch_shapes=[
                 pltpu.VMEM((4, sub_rows, LANES), F32),
                 pltpu.VMEM((2, MULTIPLES * sub_rows, LANES), F32),
@@ -489,19 +488,19 @@
                 pltpu.SMEM((32, LANES), jnp.int32),
                 pltpu.SemaphoreType.DMA(()),
             ],
-            input_output_aliases={3: 0} if before else {},
+            input_output_aliases={4: 1} if before else {},
             cost_estimate=pl.CostEstimate(
                 flops=40_000_000, bytes_accessed=8_000_000, transcendentals=0
             ),
             compiler_params=pltpu.CompilerParams(vmem_limit_bytes=16 * 1024 * 1024),
         )(*operands)
 
-    packed_again, products = products_on(1)
-    halo_far = lax.ppermute(packed_again, ring, [(i, i + 1) for i in range(1, 31, 2)])
-    (products,) = products_on(0, products)
+    packed_far, products = products_on(1)
+    halo_far = lax.ppermute(packed_far, ring, [(i, i + 1) for i in range(1, 31, 2)])
+    packed_near, products = products_on(0, products)
+    halo_near = lax.ppermute(packed_near, ring, [(i, i + 1) for i in range(0, 31, 2)])
     before, head, columns, toeplitz = kernel(
         own_kernel,
-        "own_epochs",
         (
             jax.ShapeDtypeStruct((panel + 16, panel), F32),
             jax.ShapeDtypeStruct((2, panel + 16, TAPS), BF16),
@@ -522,7 +521,6 @@
         functools.partial(
             edge_kernel, row_scale=1.0 / rows_total, gram_scale=1.0 / math.sqrt(rows_total)
         ),
-        "edge_epochs",
         jax.ShapeDtypeStruct((32, 72, LANES), BF16),
         [
             pltpu.VMEM((2, panel + 16, TAPS), BF16),
@@ -537,13 +535,10 @@
         (halo_near, halo_far, start, before, head, columns, toeplitz),
     )
     arrived = lax.all_to_all(payload, ("y", "x", "core"), 0, 0)
-    sums = kernel(
-        middle_kernel, "sum_over_plane", jax.ShapeDtypeStruct((48, 4, LANES), BF16), [], 8, (arrived,)
-    )
+    sums = kernel(middle_kernel, jax.ShapeDtypeStruct((48, 4, LANES), BF16), [], 8, (arrived,))
     gathered = lax.all_to_all(sums, ("zl", "zh"), 0, 0, tiled=True)
     normal, right_side, diagonal = kernel(
         last_kernel,
-        "sum_over_z",
         (
             jax.ShapeDtypeStruct((16, 32), F32),
             jax.ShapeDtypeStruct((1, panel), F32),

time: 62.8 us -> 65.3 us (1.040)
  starting transfers between devices: 3.38 us -> 6.23 us
    ppermute x2, starting transfers between devices: 3.38 us -> 6.23 us  [the longest x1 4.94 us: on_device(): lax.ppermute(packed_far, ring, [(i, i + 1) for i in range(1, 31, 2)])]
  transfers between devices with their start and end apart: 2 -> 2, of which waited for: 0 -> 0; matrix products, arithmetic and copies ran while one was open for 0% -> 0% of each run, Pallas kernels for 12% -> 7%
where the time goes in v7:
time: 65.3 us; the launch traced here: 65 us
  blocking collectives  46.2 us (71%)
  Pallas kernels  11.9 us (18%)
  starting transfers between devices  6.23 us (10%)
  between operations  0.7 us (1%)
    all_to_all x1, blocking collectives, on_device(): arrived = lax.all_to_all(payload, ('y', 'x', 'core'), 0, 0)  24.5 us
    all_to_all x1, blocking collectives, on_device(): gathered = lax.all_to_all(sums, ('zl', 'zh'), 0, 0, tiled=True)  21.7 us
    pallas_call x4, Pallas kernels, kernel(): pl.pallas_call(body, out_shape=outs, in_specs=[vmem] * len(operands), out...  8.06 us
    ppermute x1, starting transfers between devices, on_device(): lax.ppermute(packed_far, ring, [(i, i + 1) for i in range(1, 31, 2)])  4.94 us
    pallas_call x2, Pallas kernels, products_on(): pl.pallas_call(functools.partial(products_kernel, core=core), out_shape=o...  2.9 us
  transfers between devices with their start and end apart: 2, of which 0 were waited for; matrix products, arithmetic and copies ran while one was open for 0% of the time, Pallas kernels for 7%

profile of v7, /device:TPU:1, one launch (start us, length us, event | category | flops | bytes accessed | tf_op | source)
XLA Modules:
  0.0 65.0 jit_solution(2212127927514396157)
XLA Ops:
  0.6 0.9 %load_and_pack.1 = (f32[16,128]{1,0:T(8,128)S(1)}, s32[32,128]{1,0:T(8,128)S(1)}, f32[16,128]{1,0:T(8,128)S(1)}, f32[16,128]{1,0:T(8,128)S(1)}, bf16[2,2048]{1,0...) custom-call(f32[16,128]{1,0:T(8,128)} %bitcast.5, f32[16,128]{1,0:T(8,128)} %bitcast.6, ...), custom_call_target="tpu_custom_call" | custom-call | tf_op jit(solution)/shard_map/load_and_pack/pallas_call | solution.py:456
  1.5 2.9 %shard_map.85 = (f32[16,128]{1,0:T(8,128)S(1)}, f32[2,4,2048,128]{3,2,1,0:T(8,128)S(1)}) custom-call(f32[16,128]{1,0:T(8,128)S(1)} %get-tuple-element.22.refs_0_, f32[16,128]{1,0:T(8,128)S(1)} %get-tuple-element.23.refs_1_, s32[32,128]{1,0:T(8,128)S(1)} %get-tuple-element.24.refs_2_, f32[16,128]{1,0:T(8,128)S(1)} %get-tuple-element.25.refs_3_), custom_call_target="tpu_custom_call" | custom-call | flops 40000000 | bytes 8000000 | tf_op jit(solution)/shard_map/pallas_call | solution.py:478
  4.5 1.3 %collective-permute-start = (f32[16,128]{1,0:T(8,128)S(1)}, f32[16,128]{1,0:T(8,128)S(1)}, u32[]{:S(2)}, u32[]{:S(2)}) collective-permute-start(f32[16,128]{1,0:T(8,128)S(1)} %get-tuple-element.27), channel_id=1, source_target_pairs={{0,1},{2,3},{4,5},{6,7},{8,9},{10,11},{12,13},{14,15},{16,17},{18,... | collective-permute-start | bytes 24584 | tf_op jit(solution)/shard_map/ppermute | solution.py:501
  5.8 4.9 %collective-permute-start.1 = (f32[16,128]{1,0:T(8,128)S(1)}, f32[16,128]{1,0:T(8,128)S(1)}, u32[]{:S(2)}, u32[]{:S(2)}) collective-permute-start(f32[16,128]{1,0:T(8,128)S(1)} %get-tuple-element.28), channel_id=1, source_target_pairs={{1,2},{3,4},{5,6},{7,8},{9,10},{11,12},{13,14},{15,16},{17,18},{19... | collective-permute-start | bytes 24584 | tf_op jit(solution)/shard_map/ppermute | solution.py:499
  10.7 4.8 %shard_map.87 = (f32[528,512]{1,0:T(8,128)S(1)}, bf16[2,528,256]{2,1,0:T(8,128)(2,1)S(1)}, f32[3,512,128]{2,1,0:T(8,128)S(1)}, f32[2,3,128,128]{3,2,1,0:T(8,128)S(1)}) custom-call(f32[2,4,2048,128]{3,2,1,0:T(8,128)S(1)} %get-tuple-element.30.products, bf16[2,2048]{1,0:T(2,128)(2,1)S(1)} %get-tuple-element.31.obs_ref, ...), custom_call_target="tpu_custom_call" | custom-call | flops 4000000000 | bytes 4000000 | tf_op jit(solution)/shard_map/pallas_call | solution.py:442
  15.5 0.0 collective-permute-done.near_ref
  15.5 0.0 collective-permute-done.1.far_ref
  15.5 2.4 %shard_map.88 = bf16[32,72,128]{2,1,0:T(8,128)(2,1)S(1)} custom-call(f32[16,128]{1,0:T(8,128)S(1)} %collective-permute-done.near_ref, f32[16,128]{1,0:T(8,128)S(1)} %collective-permute-done.1.far_ref, s32[16,128]{1,0:T(8,128)S(1)} %get-tuple-element.29.start_ref, f32[528,512]{1,0:T(8,128)S(1)} %get-tuple-element.34.before_ref, ...), custom_call_target="tpu_custom_call" | custom-call | tf_op jit(solution)/shard_map/pallas_call | solution.py:442
  17.9 24.5 %all_to_all.10.in_ref = bf16[32,72,128]{2,1,0:T(8,128)(2,1)S(1)} all-to-all(bf16[32,72,128]{2,1,0:T(8,128)(2,1)S(1)} %shard_map.88), channel_id=1, replica_groups=mesh['zl'=4,'y'=4,'zh'=4,'x'=4,'core'=2] {'y','x','core'}, dimensions={0} | all-to-all | bytes 1179648 | tf_op jit(solution)/shard_map/all_to_all | solution.py:537
  42.4 0.2 shard_map.89
  42.6 21.7 %all_to_all.11.in_ref = bf16[48,4,128]{2,1,0:T(4,128)(2,1)S(1)} all-to-all(bf16[48,4,128]{2,1,0:T(4,128)(2,1)S(1)} %shard_map.89), channel_id=1, replica_groups=mesh['zl'=4,'y'=4,'zh'=4,'x'=4,'core'=2] {'zl','zh'}, dimensions={0} | all-to-all | bytes 98304 | tf_op jit(solution)/shard_map/all_to_all | solution.py:539
  64.3 0.7 %shard_map.90 = (f32[16,32]{1,0:T(8,128)}, f32[1,512]{1,0:T(1,128)}, f32[1,512]{1,0:T(1,128)}) custom-call(bf16[48,4,128]{2,1,0:T(4,128)(2,1)S(1)} %all_to_all.11.in_ref), custom_call_target="tpu_custom_call" | custom-call | tf_op jit(solution)/shard_map/pallas_call | solution.py:442
  (1 shorter events, 0.0 us)
Async XLA Ops:
  4.5 11.0 %collective-permute-start = (f32[16,128]{1,0:T(8,128)S(1)}, f32[16,128]{1,0:T(8,128)S(1)}, u32[]{:S(2)}, u32[]{:S(2)}) collective-permute-start(f32[16,128]{1,0:T(8,128)S(1)} %get-tuple-element.27), channel_id=1, source_target_pairs={{0,1},{2,3},{4,5},{6,7},{8,9},{10,11},{12,13},{14,15},{16,17},{18,... | collective-permute-start | bytes 24584 | tf_op jit(solution)/shard_map/ppermute | solution.py:501
  5.8 9.7 %collective-permute-start.1 = (f32[16,128]{1,0:T(8,128)S(1)}, f32[16,128]{1,0:T(8,128)S(1)}, u32[]{:S(2)}, u32[]{:S(2)}) collective-permute-start(f32[16,128]{1,0:T(8,128)S(1)} %get-tuple-element.28), channel_id=1, source_target_pairs={{1,2},{3,4},{5,6},{7,8},{9,10},{11,12},{13,14},{15,16},{17,18},{19... | collective-permute-start | bytes 24584 | tf_op jit(solution)/shard_map/ppermute | solution.py:499

commit v8 on v7

--- a/solution.py
+++ b/solution.py
@@ -161,21 +161,25 @@
     return by_lane, by_sublane
 
 
-def fill_matrices(matrices, block, first_row, by_lane, by_sublane, toeplitz):
+def filter_matrices(first_row, by_lane, by_sublane, toeplitz):
     square = (LANES, LANES)
+    parts = ([], [])
     for sb in range(4):
         left = jnp.broadcast_to(by_sublane[:, first_row + sb : first_row + sb + 1], square)
+        across = ([], [])
         for tb in range(2):
             d = tb - sb + 2
-            place = (slice(sb * LANES, (sb + 1) * LANES), slice(tb * LANES, (tb + 1) * LANES))
+            same = None
             if 0 <= d <= 2:
                 same = left == by_lane[first_row + 2 + tb : first_row + 3 + tb, :]
-                for component in range(2):
+            for component in range(2):
+                kept = jnp.zeros(square, F32)
+                if same is not None:
                     kept = jnp.where(same, toeplitz(component, d), 0.0)
-                    matrices[block, component, place[0], place[1]] = kept.astype(BF16)
-            else:
-                for component in range(2):
-                    matrices[block, component, place[0], place[1]] = jnp.zeros(square, BF16)
+                across[component].append(kept.astype(BF16))
+        for component in range(2):
+            parts[component].append(jnp.concatenate(across[component], axis=1))
+    return [jnp.concatenate(part, axis=0) for part in parts]
 
 
 def products_kernel(
@@ -218,7 +222,6 @@
     toeplitz_ref,
     design,
     filtered,
-    matrices,
     starts,
 ):
     rows, _ = start_ref.shape
@@ -264,13 +267,11 @@
         head_ref[component] = design[component, :, 0:TAPS]
     for block in range(blocks - 1):
         to_lanes(block + 1)
-        fill_matrices(
-            matrices, block, 2 * block, by_lane, by_sublane, lambda c, d: toeplitz_ref[c, d]
-        )
+        filters = filter_matrices(2 * block, by_lane, by_sublane, lambda c, d: toeplitz_ref[c, d])
         for component in range(2):
             window = design[component, :, block * TAPS : block * TAPS + 2 * TAPS]
             low = (component * (blocks - 1) + block) * TAPS
-            filtered[:, low : low + TAPS] = dot_nn(window, matrices[block, component]).astype(BF16)
+            filtered[:, low : low + TAPS] = dot_nn(window, filters[component]).astype(BF16)
     upper, lower = three_quadrants(filtered, panel)
     half = panel // 2
     gram_ref[0 : half + 16, :] = upper
@@ -288,7 +289,6 @@
     out_ref,
     design,
     filtered,
-    matrices,
     turns,
     starts,
     gram,
@@ -310,15 +310,15 @@
     lonely = 1.0 - halo_ref[10:11, :]
     by_lane = by_lane + jnp.where(iota(square, 0) >= 2, lonely, 0.0)
     by_sublane = by_sublane + jnp.where(iota(square, 1) >= 2, lonely, 0.0)
-    fill_matrices(matrices, 0, 0, by_lane, by_sublane, lambda c, d: toeplitz_ref[c, d])
+    filters = filter_matrices(0, by_lane, by_sublane, lambda c, d: toeplitz_ref[c, d])
 
     fill_design(design, columns_ref, turns, 2)
     for component in range(2):
         low = 4 + 2 * component
         halo = jnp.concatenate([halo_ref[low : low + 1, :], halo_ref[low + 1 : low + 2, :]], axis=1)
         fill_signal(design, component, panel, halo)
-        sums = dot_nn(design[component], matrices[0, component, 0:TAPS, :]) + dot_nn(
-            head_ref[component], matrices[0, component, TAPS : 2 * TAPS, :]
+        sums = dot_nn(design[component], filters[component][0:TAPS, :]) + dot_nn(
+            head_ref[component], filters[component][TAPS : 2 * TAPS, :]
         )
         filtered[:, component * TAPS : (component + 1) * TAPS] = sums.astype(BF16)
 
@@ -433,7 +433,6 @@
 def on_device(colatitude, longitude, observed, filter_taps, segment_start, harmonic):
     rows_here = colatitude.shape[0]
     panel = harmonic.shape[1]
-    blocks = rows_here // TAPS
     rows_total = rows_here * 512
     vmem = pl.BlockSpec(memory_space=pltpu.VMEM)
     hbm = pl.BlockSpec(memory_space=pltpu.HBM)
@@ -510,7 +509,6 @@
         [
             pltpu.VMEM((2, panel + 16, rows_here), BF16),
             pltpu.VMEM((panel + 16, 2 * (rows_here - TAPS)), BF16),
-            pltpu.VMEM((blocks - 1, 2, 2 * TAPS, TAPS), BF16),
             pltpu.VMEM((LANES, LANES), F32),
         ],
         24,
@@ -525,7 +523,6 @@
         [
             pltpu.VMEM((2, panel + 16, TAPS), BF16),
             pltpu.VMEM((panel + 16, 2 * TAPS), BF16),
-            pltpu.VMEM((1, 2, 2 * TAPS, TAPS), BF16),
             pltpu.VMEM((4, 8, LANES), F32),
             pltpu.VMEM((LANES, LANES), F32),
             pltpu.VMEM((panel + 16, panel), F32),

time: 65.3 us -> 65.3 us (level)
  no operation moved by 1% of the time
where the time goes in v8:
time: 65.3 us; the launch traced here: 65 us
  blocking collectives  46.6 us (71%)
  Pallas kernels  11.5 us (18%)
  starting transfers between devices  6.23 us (10%)
  between operations  0.7 us (1%)
    all_to_all x1, blocking collectives, on_device(): arrived = lax.all_to_all(payload, ('y', 'x', 'core'), 0, 0)  24.5 us
    all_to_all x1, blocking collectives, on_device(): gathered = lax.all_to_all(sums, ('zl', 'zh'), 0, 0, tiled=True)  22.1 us
    pallas_call x4, Pallas kernels, kernel(): pl.pallas_call(body, out_shape=outs, in_specs=[vmem] * len(operands), out...  7.67 us
    ppermute x1, starting transfers between devices, on_device(): lax.ppermute(packed_far, ring, [(i, i + 1) for i in range(1, 31, 2)])  4.94 us
    pallas_call x2, Pallas kernels, products_on(): pl.pallas_call(functools.partial(products_kernel, core=core), out_shape=o...  2.9 us
  transfers between devices with their start and end apart: 2, of which 0 were waited for; matrix products, arithmetic and copies ran while one was open for 0% of the time, Pallas kernels for 7%

profile of v8, /device:TPU:1, one launch (start us, length us, event | category | flops | bytes accessed | tf_op | source)
XLA Modules:
  0.0 65.0 jit_solution(17552615013277071924)
XLA Ops:
  0.6 0.9 %load_and_pack.1 = (f32[16,128]{1,0:T(8,128)S(1)}, s32[32,128]{1,0:T(8,128)S(1)}, f32[16,128]{1,0:T(8,128)S(1)}, f32[16,128]{1,0:T(8,128)S(1)}, bf16[2,2048]{1,0...) custom-call(f32[16,128]{1,0:T(8,128)} %bitcast.5, f32[16,128]{1,0:T(8,128)} %bitcast.6, ...), custom_call_target="tpu_custom_call" | custom-call | tf_op jit(solution)/shard_map/load_and_pack/pallas_call | solution.py:455
  1.5 2.9 %shard_map.85 = (f32[16,128]{1,0:T(8,128)S(1)}, f32[2,4,2048,128]{3,2,1,0:T(8,128)S(1)}) custom-call(f32[16,128]{1,0:T(8,128)S(1)} %get-tuple-element.22.refs_0_, f32[16,128]{1,0:T(8,128)S(1)} %get-tuple-element.23.refs_1_, s32[32,128]{1,0:T(8,128)S(1)} %get-tuple-element.24.refs_2_, f32[16,128]{1,0:T(8,128)S(1)} %get-tuple-element.25.refs_3_), custom_call_target="tpu_custom_call" | custom-call | flops 40000000 | bytes 8000000 | tf_op jit(solution)/shard_map/pallas_call | solution.py:477
  4.5 1.3 %collective-permute-start = (f32[16,128]{1,0:T(8,128)S(1)}, f32[16,128]{1,0:T(8,128)S(1)}, u32[]{:S(2)}, u32[]{:S(2)}) collective-permute-start(f32[16,128]{1,0:T(8,128)S(1)} %get-tuple-element.27), channel_id=1, source_target_pairs={{0,1},{2,3},{4,5},{6,7},{8,9},{10,11},{12,13},{14,15},{16,17},{18,... | collective-permute-start | bytes 24584 | tf_op jit(solution)/shard_map/ppermute | solution.py:500
  5.8 4.9 %collective-permute-start.1 = (f32[16,128]{1,0:T(8,128)S(1)}, f32[16,128]{1,0:T(8,128)S(1)}, u32[]{:S(2)}, u32[]{:S(2)}) collective-permute-start(f32[16,128]{1,0:T(8,128)S(1)} %get-tuple-element.28), channel_id=1, source_target_pairs={{1,2},{3,4},{5,6},{7,8},{9,10},{11,12},{13,14},{15,16},{17,18},{19... | collective-permute-start | bytes 24584 | tf_op jit(solution)/shard_map/ppermute | solution.py:498
  10.7 4.4 %shard_map.87 = (f32[528,512]{1,0:T(8,128)S(1)}, bf16[2,528,256]{2,1,0:T(8,128)(2,1)S(1)}, f32[3,512,128]{2,1,0:T(8,128)S(1)}, f32[2,3,128,128]{3,2,1,0:T(8,128)S(1)}) custom-call(f32[2,4,2048,128]{3,2,1,0:T(8,128)S(1)} %get-tuple-element.30.products, bf16[2,2048]{1,0:T(2,128)(2,1)S(1)} %get-tuple-element.31.obs_ref, ...), custom_call_target="tpu_custom_call" | custom-call | flops 4000000000 | bytes 4000000 | tf_op jit(solution)/shard_map/pallas_call | solution.py:441
  15.1 0.0 collective-permute-done.near_ref
  15.1 0.0 collective-permute-done.1.far_ref
  15.1 2.4 %shard_map.88 = bf16[32,72,128]{2,1,0:T(8,128)(2,1)S(1)} custom-call(f32[16,128]{1,0:T(8,128)S(1)} %collective-permute-done.near_ref, f32[16,128]{1,0:T(8,128)S(1)} %collective-permute-done.1.far_ref, s32[16,128]{1,0:T(8,128)S(1)} %get-tuple-element.29.start_ref, f32[528,512]{1,0:T(8,128)S(1)} %get-tuple-element.34.before_ref, ...), custom_call_target="tpu_custom_call" | custom-call | tf_op jit(solution)/shard_map/pallas_call | solution.py:441
  17.5 24.5 %all_to_all.10.in_ref = bf16[32,72,128]{2,1,0:T(8,128)(2,1)S(1)} all-to-all(bf16[32,72,128]{2,1,0:T(8,128)(2,1)S(1)} %shard_map.88), channel_id=1, replica_groups=mesh['zl'=4,'y'=4,'zh'=4,'x'=4,'core'=2] {'y','x','core'}, dimensions={0} | all-to-all | bytes 1179648 | tf_op jit(solution)/shard_map/all_to_all | solution.py:534
  42.0 0.2 shard_map.89
  42.2 22.1 %all_to_all.11.in_ref = bf16[48,4,128]{2,1,0:T(4,128)(2,1)S(1)} all-to-all(bf16[48,4,128]{2,1,0:T(4,128)(2,1)S(1)} %shard_map.89), channel_id=1, replica_groups=mesh['zl'=4,'y'=4,'zh'=4,'x'=4,'core'=2] {'zl','zh'}, dimensions={0} | all-to-all | bytes 98304 | tf_op jit(solution)/shard_map/all_to_all | solution.py:536
  64.3 0.7 %shard_map.90 = (f32[16,32]{1,0:T(8,128)}, f32[1,512]{1,0:T(1,128)}, f32[1,512]{1,0:T(1,128)}) custom-call(bf16[48,4,128]{2,1,0:T(4,128)(2,1)S(1)} %all_to_all.11.in_ref), custom_call_target="tpu_custom_call" | custom-call | tf_op jit(solution)/shard_map/pallas_call | solution.py:441
  (1 shorter events, 0.0 us)
Async XLA Ops:
  4.5 10.6 %collective-permute-start = (f32[16,128]{1,0:T(8,128)S(1)}, f32[16,128]{1,0:T(8,128)S(1)}, u32[]{:S(2)}, u32[]{:S(2)}) collective-permute-start(f32[16,128]{1,0:T(8,128)S(1)} %get-tuple-element.27), channel_id=1, source_target_pairs={{0,1},{2,3},{4,5},{6,7},{8,9},{10,11},{12,13},{14,15},{16,17},{18,... | collective-permute-start | bytes 24584 | tf_op jit(solution)/shard_map/ppermute | solution.py:500
  5.8 9.3 %collective-permute-start.1 = (f32[16,128]{1,0:T(8,128)S(1)}, f32[16,128]{1,0:T(8,128)S(1)}, u32[]{:S(2)}, u32[]{:S(2)}) collective-permute-start(f32[16,128]{1,0:T(8,128)S(1)} %get-tuple-element.28), channel_id=1, source_target_pairs={{1,2},{3,4},{5,6},{7,8},{9,10},{11,12},{13,14},{15,16},{17,18},{19... | collective-permute-start | bytes 24584 | tf_op jit(solution)/shard_map/ppermute | solution.py:498

commit v9 on v8

--- a/solution.py
+++ b/solution.py
@@ -102,16 +102,18 @@
             small[slot, 0, b] = cosine
             small[slot, 1, b] = sine
 
-    def some_multiples(a, carry):
-        for slot, table in enumerate(tables):
-            sine, cosine = sine_and_cosine(turns, slot, (16 * a).astype(F32))
-            for b in range(16):
-                place = pl.ds(pl.multiple_of(a * (16 * rows), 16 * rows) + b * rows, rows)
-                table[0, place, :] = cosine * small[slot, 0, b] - sine * small[slot, 1, b]
-                table[1, place, :] = sine * small[slot, 0, b] + cosine * small[slot, 1, b]
+    def some_multiples(step, carry):
+        for a in range(3):
+            first = 3 * step + a
+            for slot, table in enumerate(tables):
+                sine, cosine = sine_and_cosine(turns, slot, (16 * first).astype(F32))
+                for b in range(16):
+                    place = pl.ds(pl.multiple_of(first * (16 * rows), 16 * rows) + b * rows, rows)
+                    table[0, place, :] = cosine * small[slot, 0, b] - sine * small[slot, 1, b]
+                    table[1, place, :] = sine * small[slot, 0, b] + cosine * small[slot, 1, b]
         return carry
 
-    lax.fori_loop(0, MULTIPLES // 16, some_multiples, 0)
+    lax.fori_loop(0, MULTIPLES // 48, some_multiples, 0)
 
 
 def fill_products(products, rows_of, tables):
@@ -293,9 +295,6 @@
     starts,
     gram,
     halo_ref,
-    *,
-    row_scale,
-    gram_scale,
 ):
     panel = columns_ref.shape[1]
     halo_ref[...] = near_ref[...] + far_ref[...]
@@ -331,14 +330,13 @@
     gram[half:panel, 0:half] = jnp.transpose(upper[0:half, half:panel])
 
     eye = iota(square, 0) == iota(square, 1)
-    rhs = [gram[panel : panel + 1, y * LANES : (y + 1) * LANES] * gram_scale for y in range(4)]
+    rhs = [gram[panel : panel + 1, y * LANES : (y + 1) * LANES] for y in range(4)]
     diagonal = [
         jnp.sum(
             jnp.where(eye, gram[y * LANES : (y + 1) * LANES, y * LANES : (y + 1) * LANES], 0.0),
             axis=0,
             keepdims=True,
         )
-        * row_scale
         for y in range(4)
     ]
     small = jnp.concatenate(rhs + diagonal, axis=0).astype(BF16)
@@ -348,9 +346,9 @@
                 peer = y * 8 + x * 2 + core
                 for zh in range(4):
                     low = x * 128 + zh * 32 + core * 16
-                    out_ref[peer, zh * 16 : zh * 16 + 16, :] = (
-                        gram[low : low + 16, y * LANES : (y + 1) * LANES] * gram_scale
-                    ).astype(BF16)
+                    out_ref[peer, zh * 16 : zh * 16 + 16, :] = gram[
+                        low : low + 16, y * LANES : (y + 1) * LANES
+                    ].astype(BF16)
                 out_ref[peer, 64:72, :] = small
 
 
@@ -370,13 +368,13 @@
             out_ref[low + 2] = rounded[68:72, :]
 
 
-def last_kernel(in_ref, normal_ref, rhs_ref, diagonal_ref):
+def last_kernel(in_ref, normal_ref, rhs_ref, diagonal_ref, *, row_scale, gram_scale):
     totals = []
     for part in range(3):
         total = in_ref[part].astype(F32)
         for peer in range(1, in_ref.shape[0] // 3):
             total = total + in_ref[3 * peer + part].astype(F32)
-        totals.append(total)
+        totals.append(total * (gram_scale, gram_scale, row_scale)[part])
     for b in range(4):
         normal_ref[4 * b : 4 * b + 4, :] = totals[0][:, b * 32 : b * 32 + 32]
     rows, cols = normal_ref.shape
@@ -516,9 +514,7 @@
         pl.CostEstimate(flops=4_000_000_000, bytes_accessed=4_000_000, transcendentals=0),
     )
     payload = kernel(
-        functools.partial(
-            edge_kernel, row_scale=1.0 / rows_total, gram_scale=1.0 / math.sqrt(rows_total)
-        ),
+        edge_kernel,
         jax.ShapeDtypeStruct((32, 72, LANES), BF16),
         [
             pltpu.VMEM((2, panel + 16, TAPS), BF16),
@@ -535,7 +531,9 @@
     sums = kernel(middle_kernel, jax.ShapeDtypeStruct((48, 4, LANES), BF16), [], 8, (arrived,))
     gathered = lax.all_to_all(sums, ("zl", "zh"), 0, 0, tiled=True)
     normal, right_side, diagonal = kernel(
-        last_kernel,
+        functools.partial(
+            last_kernel, row_scale=1.0 / rows_total, gram_scale=1.0 / math.sqrt(rows_total)
+        ),
         (
             jax.ShapeDtypeStruct((16, 32), F32),
             jax.ShapeDtypeStruct((1, panel), F32),

time: 65.3 us -> 65.1 us (level)
  no operation moved by 1% of the time
where the time goes in v9:
time: 65.1 us; the launch traced here: 64.8 us
  blocking collectives  46.6 us (72%)
  Pallas kernels  11.3 us (17%)
  starting transfers between devices  6.23 us (10%)
  between operations  0.7 us (1%)
    all_to_all x1, blocking collectives, on_device(): arrived = lax.all_to_all(payload, ('y', 'x', 'core'), 0, 0)  24.5 us
    all_to_all x1, blocking collectives, on_device(): gathered = lax.all_to_all(sums, ('zl', 'zh'), 0, 0, tiled=True)  22.1 us
    pallas_call x4, Pallas kernels, kernel(): pl.pallas_call(body, out_shape=outs, in_specs=[vmem] * len(operands), out...  7.68 us
    ppermute x1, starting transfers between devices, on_device(): lax.ppermute(packed_far, ring, [(i, i + 1) for i in range(1, 31, 2)])  4.94 us
    pallas_call x2, Pallas kernels, products_on(): pl.pallas_call(functools.partial(products_kernel, core=core), out_shape=o...  2.69 us
  transfers between devices with their start and end apart: 2, of which 0 were waited for; matrix products, arithmetic and copies ran while one was open for 0% of the time, Pallas kernels for 7%

profile of v9, /device:TPU:1, one launch (start us, length us, event | category | flops | bytes accessed | tf_op | source)
XLA Modules:
  0.0 64.8 jit_solution(15119277602153682976)
XLA Ops:
  0.6 0.9 %load_and_pack.1 = (f32[16,128]{1,0:T(8,128)S(1)}, s32[32,128]{1,0:T(8,128)S(1)}, f32[16,128]{1,0:T(8,128)S(1)}, f32[16,128]{1,0:T(8,128)S(1)}, bf16[2,2048]{1,0...) custom-call(f32[16,128]{1,0:T(8,128)} %bitcast.5, f32[16,128]{1,0:T(8,128)} %bitcast.6, ...), custom_call_target="tpu_custom_call" | custom-call | tf_op jit(solution)/shard_map/load_and_pack/pallas_call | solution.py:453
  1.5 2.7 %shard_map.85 = (f32[16,128]{1,0:T(8,128)S(1)}, f32[2,4,2048,128]{3,2,1,0:T(8,128)S(1)}) custom-call(f32[16,128]{1,0:T(8,128)S(1)} %get-tuple-element.22.refs_0_, f32[16,128]{1,0:T(8,128)S(1)} %get-tuple-element.23.refs_1_, s32[32,128]{1,0:T(8,128)S(1)} %get-tuple-element.24.refs_2_, f32[16,128]{1,0:T(8,128)S(1)} %get-tuple-element.25.refs_3_), custom_call_target="tpu_custom_call" | custom-call | flops 40000000 | bytes 8000000 | tf_op jit(solution)/shard_map/pallas_call | solution.py:475
  4.2 1.3 %collective-permute-start = (f32[16,128]{1,0:T(8,128)S(1)}, f32[16,128]{1,0:T(8,128)S(1)}, u32[]{:S(2)}, u32[]{:S(2)}) collective-permute-start(f32[16,128]{1,0:T(8,128)S(1)} %get-tuple-element.27), channel_id=1, source_target_pairs={{0,1},{2,3},{4,5},{6,7},{8,9},{10,11},{12,13},{14,15},{16,17},{18,... | collective-permute-start | bytes 24584 | tf_op jit(solution)/shard_map/ppermute | solution.py:498
  5.5 4.9 %collective-permute-start.1 = (f32[16,128]{1,0:T(8,128)S(1)}, f32[16,128]{1,0:T(8,128)S(1)}, u32[]{:S(2)}, u32[]{:S(2)}) collective-permute-start(f32[16,128]{1,0:T(8,128)S(1)} %get-tuple-element.28), channel_id=1, source_target_pairs={{1,2},{3,4},{5,6},{7,8},{9,10},{11,12},{13,14},{15,16},{17,18},{19... | collective-permute-start | bytes 24584 | tf_op jit(solution)/shard_map/ppermute | solution.py:496
  10.5 4.4 %shard_map.87 = (f32[528,512]{1,0:T(8,128)S(1)}, bf16[2,528,256]{2,1,0:T(8,128)(2,1)S(1)}, f32[3,512,128]{2,1,0:T(8,128)S(1)}, f32[2,3,128,128]{3,2,1,0:T(8,128)S(1)}) custom-call(f32[2,4,2048,128]{3,2,1,0:T(8,128)S(1)} %get-tuple-element.30.products, bf16[2,2048]{1,0:T(2,128)(2,1)S(1)} %get-tuple-element.31.obs_ref, ...), custom_call_target="tpu_custom_call" | custom-call | flops 4000000000 | bytes 4000000 | tf_op jit(solution)/shard_map/pallas_call | solution.py:439
  14.9 0.0 collective-permute-done.near_ref
  14.9 0.0 collective-permute-done.1.far_ref
  14.9 2.4 %shard_map.88 = bf16[32,72,128]{2,1,0:T(8,128)(2,1)S(1)} custom-call(f32[16,128]{1,0:T(8,128)S(1)} %collective-permute-done.near_ref, f32[16,128]{1,0:T(8,128)S(1)} %collective-permute-done.1.far_ref, s32[16,128]{1,0:T(8,128)S(1)} %get-tuple-element.29.start_ref, f32[528,512]{1,0:T(8,128)S(1)} %get-tuple-element.34.before_ref, ...), custom_call_target="tpu_custom_call" | custom-call | tf_op jit(solution)/shard_map/pallas_call | solution.py:439
  17.3 24.5 %all_to_all.10.in_ref = bf16[32,72,128]{2,1,0:T(8,128)(2,1)S(1)} all-to-all(bf16[32,72,128]{2,1,0:T(8,128)(2,1)S(1)} %shard_map.88), channel_id=1, replica_groups=mesh['zl'=4,'y'=4,'zh'=4,'x'=4,'core'=2] {'y','x','core'}, dimensions={0} | all-to-all | bytes 1179648 | tf_op jit(solution)/shard_map/all_to_all | solution.py:530
  41.8 0.2 shard_map.89
  42.0 22.1 %all_to_all.11.in_ref = bf16[48,4,128]{2,1,0:T(4,128)(2,1)S(1)} all-to-all(bf16[48,4,128]{2,1,0:T(4,128)(2,1)S(1)} %shard_map.89), channel_id=1, replica_groups=mesh['zl'=4,'y'=4,'zh'=4,'x'=4,'core'=2] {'zl','zh'}, dimensions={0} | all-to-all | bytes 98304 | tf_op jit(solution)/shard_map/all_to_all | solution.py:532
  64.1 0.7 %shard_map.90 = (f32[16,32]{1,0:T(8,128)}, f32[1,512]{1,0:T(1,128)}, f32[1,512]{1,0:T(1,128)}) custom-call(bf16[48,4,128]{2,1,0:T(4,128)(2,1)S(1)} %all_to_all.11.in_ref), custom_call_target="tpu_custom_call" | custom-call | tf_op jit(solution)/shard_map/pallas_call | solution.py:439
  (1 shorter events, 0.0 us)
Async XLA Ops:
  4.2 10.6 %collective-permute-start = (f32[16,128]{1,0:T(8,128)S(1)}, f32[16,128]{1,0:T(8,128)S(1)}, u32[]{:S(2)}, u32[]{:S(2)}) collective-permute-start(f32[16,128]{1,0:T(8,128)S(1)} %get-tuple-element.27), channel_id=1, source_target_pairs={{0,1},{2,3},{4,5},{6,7},{8,9},{10,11},{12,13},{14,15},{16,17},{18,... | collective-permute-start | bytes 24584 | tf_op jit(solution)/shard_map/ppermute | solution.py:498
  5.5 9.3 %collective-permute-start.1 = (f32[16,128]{1,0:T(8,128)S(1)}, f32[16,128]{1,0:T(8,128)S(1)}, u32[]{:S(2)}, u32[]{:S(2)}) collective-permute-start(f32[16,128]{1,0:T(8,128)S(1)} %get-tuple-element.28), channel_id=1, source_target_pairs={{1,2},{3,4},{5,6},{7,8},{9,10},{11,12},{13,14},{15,16},{17,18},{19... | collective-permute-start | bytes 24584 | tf_op jit(solution)/shard_map/ppermute | solution.py:496

commit v10 on v9

--- a/solution.py
+++ b/solution.py
@@ -96,19 +96,29 @@
 
 def fill_tables(tables, turns, small):
     rows = turns.shape[1]
+
+    def added(one, two):
+        return one[0] * two[1] + one[1] * two[0], one[1] * two[1] - one[0] * two[0]
+
     for slot in range(2):
+        few = {b: sine_and_cosine(turns, slot, float(b)) for b in (0, 1, 2, 3, 4, 8, 12, 16, 32)}
         for b in range(16):
-            sine, cosine = sine_and_cosine(turns, slot, float(b))
+            sine, cosine = few[b] if b in few else added(few[b // 4 * 4], few[b % 4])
             small[slot, 0, b] = cosine
             small[slot, 1, b] = sine
+        for index, b in ((16, 16), (17, 32)):
+            small[slot, 0, index] = few[b][1]
+            small[slot, 1, index] = few[b][0]
 
     def some_multiples(step, carry):
-        for a in range(3):
-            first = 3 * step + a
-            for slot, table in enumerate(tables):
-                sine, cosine = sine_and_cosine(turns, slot, (16 * first).astype(F32))
+        for slot, table in enumerate(tables):
+            first = sine_and_cosine(turns, slot, (48 * step).astype(F32))
+            for a in range(3):
+                sine, cosine = first
+                if a:
+                    sine, cosine = added(first, (small[slot, 1, 15 + a], small[slot, 0, 15 + a]))
                 for b in range(16):
-                    place = pl.ds(pl.multiple_of(first * (16 * rows), 16 * rows) + b * rows, rows)
+                    place = pl.ds(pl.multiple_of(step * (48 * rows), 48 * rows) + (16 * a + b) * rows, rows)
                     table[0, place, :] = cosine * small[slot, 0, b] - sine * small[slot, 1, b]
                     table[1, place, :] = sine * small[slot, 0, b] + cosine * small[slot, 1, b]
         return carry
@@ -481,7 +491,7 @@
                 pltpu.VMEM((4, sub_rows, LANES), F32),
                 pltpu.VMEM((2, MULTIPLES * sub_rows, LANES), F32),
                 pltpu.VMEM((2 * MULTIPLES * sub_rows, LANES), F32),
-                pltpu.VMEM((2, 2, 16, sub_rows, LANES), F32),
+                pltpu.VMEM((2, 2, 18, sub_rows, LANES), F32),
                 pltpu.SMEM((32, LANES), jnp.int32),
                 pltpu.SemaphoreType.DMA(()),
             ],

time: 65.1 us -> 64.9 us (level)
  no operation moved by 1% of the time
where the time goes in v10:
time: 64.9 us; the launch traced here: 64.7 us
  blocking collectives  46.6 us (72%)
  Pallas kernels  11.1 us (17%)
  starting transfers between devices  6.23 us (10%)
  between operations  0.7 us (1%)
    all_to_all x1, blocking collectives, on_device(): arrived = lax.all_to_all(payload, ('y', 'x', 'core'), 0, 0)  24.5 us
    all_to_all x1, blocking collectives, on_device(): gathered = lax.all_to_all(sums, ('zl', 'zh'), 0, 0, tiled=True)  22.1 us
    pallas_call x4, Pallas kernels, kernel(): pl.pallas_call(body, out_shape=outs, in_specs=[vmem] * len(operands), out...  7.67 us
    ppermute x1, starting transfers between devices, on_device(): lax.ppermute(packed_far, ring, [(i, i + 1) for i in range(1, 31, 2)])  4.94 us
    pallas_call x2, Pallas kernels, products_on(): pl.pallas_call(functools.partial(products_kernel, core=core), out_shape=o...  2.55 us
  transfers between devices with their start and end apart: 2, of which 0 were waited for; matrix products, arithmetic and copies ran while one was open for 0% of the time, Pallas kernels for 7%

profile of v10, /device:TPU:1, one launch (start us, length us, event | category | flops | bytes accessed | tf_op | source)
XLA Modules:
  0.0 64.7 jit_solution(7942621580854587458)
XLA Ops:
  0.6 0.9 %load_and_pack.1 = (f32[16,128]{1,0:T(8,128)S(1)}, s32[32,128]{1,0:T(8,128)S(1)}, f32[16,128]{1,0:T(8,128)S(1)}, f32[16,128]{1,0:T(8,128)S(1)}, bf16[2,2048]{1,0...) custom-call(f32[16,128]{1,0:T(8,128)} %bitcast.5, f32[16,128]{1,0:T(8,128)} %bitcast.6, ...), custom_call_target="tpu_custom_call" | custom-call | tf_op jit(solution)/shard_map/load_and_pack/pallas_call | solution.py:463
  1.5 2.5 %shard_map.85 = (f32[16,128]{1,0:T(8,128)S(1)}, f32[2,4,2048,128]{3,2,1,0:T(8,128)S(1)}) custom-call(f32[16,128]{1,0:T(8,128)S(1)} %get-tuple-element.22.refs_0_, f32[16,128]{1,0:T(8,128)S(1)} %get-tuple-element.23.refs_1_, s32[32,128]{1,0:T(8,128)S(1)} %get-tuple-element.24.refs_2_, f32[16,128]{1,0:T(8,128)S(1)} %get-tuple-element.25.refs_3_), custom_call_target="tpu_custom_call" | custom-call | flops 40000000 | bytes 8000000 | tf_op jit(solution)/shard_map/pallas_call | solution.py:485
  4.1 1.3 %collective-permute-start = (f32[16,128]{1,0:T(8,128)S(1)}, f32[16,128]{1,0:T(8,128)S(1)}, u32[]{:S(2)}, u32[]{:S(2)}) collective-permute-start(f32[16,128]{1,0:T(8,128)S(1)} %get-tuple-element.27), channel_id=1, source_target_pairs={{0,1},{2,3},{4,5},{6,7},{8,9},{10,11},{12,13},{14,15},{16,17},{18,... | collective-permute-start | bytes 24584 | tf_op jit(solution)/shard_map/ppermute | solution.py:508
  5.4 4.9 %collective-permute-start.1 = (f32[16,128]{1,0:T(8,128)S(1)}, f32[16,128]{1,0:T(8,128)S(1)}, u32[]{:S(2)}, u32[]{:S(2)}) collective-permute-start(f32[16,128]{1,0:T(8,128)S(1)} %get-tuple-element.28), channel_id=1, source_target_pairs={{1,2},{3,4},{5,6},{7,8},{9,10},{11,12},{13,14},{15,16},{17,18},{19... | collective-permute-start | bytes 24584 | tf_op jit(solution)/shard_map/ppermute | solution.py:506
  10.4 4.4 %shard_map.87 = (f32[528,512]{1,0:T(8,128)S(1)}, bf16[2,528,256]{2,1,0:T(8,128)(2,1)S(1)}, f32[3,512,128]{2,1,0:T(8,128)S(1)}, f32[2,3,128,128]{3,2,1,0:T(8,128)S(1)}) custom-call(f32[2,4,2048,128]{3,2,1,0:T(8,128)S(1)} %get-tuple-element.30.products, bf16[2,2048]{1,0:T(2,128)(2,1)S(1)} %get-tuple-element.31.obs_ref, ...), custom_call_target="tpu_custom_call" | custom-call | flops 4000000000 | bytes 4000000 | tf_op jit(solution)/shard_map/pallas_call | solution.py:449
  14.7 0.0 collective-permute-done.near_ref
  14.7 0.0 collective-permute-done.1.far_ref
  14.7 2.4 %shard_map.88 = bf16[32,72,128]{2,1,0:T(8,128)(2,1)S(1)} custom-call(f32[16,128]{1,0:T(8,128)S(1)} %collective-permute-done.near_ref, f32[16,128]{1,0:T(8,128)S(1)} %collective-permute-done.1.far_ref, s32[16,128]{1,0:T(8,128)S(1)} %get-tuple-element.29.start_ref, f32[528,512]{1,0:T(8,128)S(1)} %get-tuple-element.34.before_ref, ...), custom_call_target="tpu_custom_call" | custom-call | tf_op jit(solution)/shard_map/pallas_call | solution.py:449
  17.2 24.5 %all_to_all.10.in_ref = bf16[32,72,128]{2,1,0:T(8,128)(2,1)S(1)} all-to-all(bf16[32,72,128]{2,1,0:T(8,128)(2,1)S(1)} %shard_map.88), channel_id=1, replica_groups=mesh['zl'=4,'y'=4,'zh'=4,'x'=4,'core'=2] {'y','x','core'}, dimensions={0} | all-to-all | bytes 1179648 | tf_op jit(solution)/shard_map/all_to_all | solution.py:540
  41.6 0.2 shard_map.89
  41.8 22.1 %all_to_all.11.in_ref = bf16[48,4,128]{2,1,0:T(4,128)(2,1)S(1)} all-to-all(bf16[48,4,128]{2,1,0:T(4,128)(2,1)S(1)} %shard_map.89), channel_id=1, replica_groups=mesh['zl'=4,'y'=4,'zh'=4,'x'=4,'core'=2] {'zl','zh'}, dimensions={0} | all-to-all | bytes 98304 | tf_op jit(solution)/shard_map/all_to_all | solution.py:542
  64.0 0.7 %shard_map.90 = (f32[16,32]{1,0:T(8,128)}, f32[1,512]{1,0:T(1,128)}, f32[1,512]{1,0:T(1,128)}) custom-call(bf16[48,4,128]{2,1,0:T(4,128)(2,1)S(1)} %all_to_all.11.in_ref), custom_call_target="tpu_custom_call" | custom-call | tf_op jit(solution)/shard_map/pallas_call | solution.py:449
  (1 shorter events, 0.0 us)
Async XLA Ops:
  4.1 10.6 %collective-permute-start = (f32[16,128]{1,0:T(8,128)S(1)}, f32[16,128]{1,0:T(8,128)S(1)}, u32[]{:S(2)}, u32[]{:S(2)}) collective-permute-start(f32[16,128]{1,0:T(8,128)S(1)} %get-tuple-element.27), channel_id=1, source_target_pairs={{0,1},{2,3},{4,5},{6,7},{8,9},{10,11},{12,13},{14,15},{16,17},{18,... | collective-permute-start | bytes 24584 | tf_op jit(solution)/shard_map/ppermute | solution.py:508
  5.4 9.3 %collective-permute-start.1 = (f32[16,128]{1,0:T(8,128)S(1)}, f32[16,128]{1,0:T(8,128)S(1)}, u32[]{:S(2)}, u32[]{:S(2)}) collective-permute-start(f32[16,128]{1,0:T(8,128)S(1)} %get-tuple-element.28), channel_id=1, source_target_pairs={{1,2},{3,4},{5,6},{7,8},{9,10},{11,12},{13,14},{15,16},{17,18},{19... | collective-permute-start | bytes 24584 | tf_op jit(solution)/shard_map/ppermute | solution.py:506
